TPU v7x, 128 devices: a whole 4x4x4 slice. The times are simulated.
128 devices in a mesh: row: 8 (over y, core), col: 16 (over x, z).
Axes of the slice: x: 4, y: 4, z: 4, core: 2. Of those that a mesh axis runs over, the one named last changes fastest.
Arguments:
- rhs: float32 [512, 8192], P('col', 'row'), may hold values from -6 to 6
- couple_prev: float32 [8192, 1024], P('row'), may hold values from -0.1875 to 0.1875
- diag_inverse: float32 [8192, 1024], P('row'), may hold values from -2 to 2
- coupling: bfloat16 [1536, 16, 128], P(('row', 'col')), may hold values from -0.5 to 0.5
- pair_block: int32 [1536], P(('row', 'col')), may hold values from 0 to 63, as said below
- pair_tile: int32 [1536], P(('row', 'col')), may hold values from 0 to 2
- pair_count: int32 [128], P(('row', 'col')), may hold values from 8 to 12, as said below
- owner_slot: int32 [8, 48], P('row'), may hold values from 0 to 47, each once within a row
- schur: bfloat16 [6144, 65536], P('row', 'col'), may hold values from -6 to 6
- surface_factor: bfloat16 [512, 65536], P(None, 'col'), may hold values from -0.125 to 0.125
Outputs:
- updated: bfloat16 [6144, 65536], P('row', 'col')
Inputs may be any that keep to these rules, and one draw needn't show every extreme that they name: Among the first pair_count entries of one owner, at most 3 name blocks whose block-row group pair_block // 8 is the same; some owner has exactly 3 from one group. `pair_count`: some owner has 12 live coupling tiles.
All inputs are finite; a program needn't handle non-finite values.
Results may differ from a plain program's by a relative error of at most 0.0055.
Values may be sent and summed in bfloat16 or wider, within the bound.
No kernel may reach another device: no remote copies, remote signals or barrier semaphores. Data moves between devices by JAX's collectives and lax.ppermute only.
A program may use at most 128 MiB of HBM per device.

v0:
```python
import jax
import jax.numpy as jnp
from jax import lax
from jax.experimental import pallas as pl
from jax.experimental.pallas import tpu as pltpu
from jax.sharding import PartitionSpec as P

NB = 1024
BLK = 128
TILE = 16
TPD = 3
KCAP = 12
TPR = 48
SR = 768
NRHS = 512
N_ROW = 8
N_COL = 16
COLS = NRHS // N_COL
PER = NB // BLK
SIDE = 4
CHUNKS = 4
BF = jnp.bfloat16
F32 = jnp.float32


def split(value):
    high = value.astype(BF)
    return high, (value - high.astype(F32)).astype(BF)


def in_hbm(value):
    return pltpu.with_memory_space_constraint(value, pltpu.HBM)


def mm(left, right):
    return jnp.dot(left, right, preferred_element_type=F32)


def vmem():
    return pl.BlockSpec(memory_space=pltpu.VMEM)


def smem():
    return pl.BlockSpec(memory_space=pltpu.SMEM)


def small(limit):
    return pltpu.CompilerParams(vmem_limit_bytes=limit << 20)


def hbm():
    return pl.BlockSpec(memory_space=pltpu.HBM)


def shape(rows, kind=BF):
    return jax.ShapeDtypeStruct((rows, NB), kind)


def with_split(left, high, low):
    first, second = split(left)
    both = mm(jnp.concatenate([first, second], axis=0), high)
    return both[: left.shape[0]] + both[left.shape[0] :] + mm(first, low)


def prep_body(rhs_hbm, e_hbm, g_hbm, sent_ref, e_high, e_low, g_high, g_low, rhs_in, e_in, g_in, sems):
    rows = NB // CHUNKS
    moves = [pltpu.make_async_copy(rhs_hbm, rhs_in, sems.at[0])]
    for source, target in ((g_hbm, g_in), (e_hbm, e_in)):
        for at in range(CHUNKS):
            piece = pl.ds(at * rows, rows)
            moves.append(pltpu.make_async_copy(source.at[piece], target.at[piece], sems.at[len(moves)]))
    for move in moves:
        move.start()
    for at in range(CHUNKS):
        piece = pl.ds(at * rows, rows)
        moves[1 + at].wait()
        g_high[piece], g_low[piece] = split(g_in[piece])
    moves[0].wait()
    sent_ref[...] = with_split(rhs_in[...], g_high[...], g_low[...]).astype(BF)
    for at in range(CHUNKS):
        piece = pl.ds(at * rows, rows)
        moves[1 + CHUNKS + at].wait()
        e_high[piece], e_low[piece] = split(e_in[piece])


def prep(rhs, lower, inverse):
    return pl.pallas_call(
        prep_body,
        in_specs=[hbm()] * 3,
        out_specs=[vmem()] * 5,
        out_shape=[shape(COLS)] + [shape(NB)] * 4,
        scratch_shapes=[
            pltpu.VMEM((COLS, NB), F32),
            pltpu.VMEM((NB, NB), F32),
            pltpu.VMEM((NB, NB), F32),
            pltpu.SemaphoreType.DMA((1 + 2 * CHUNKS,)),
        ],
        compiler_params=small(12),
        name="prep",
    )(in_hbm(rhs), in_hbm(lower), in_hbm(inverse))


def advance(step, sent, before, rhs, factors):
    def body(sent_ref, rhs_ref, before_ref, e_high, e_low, g_high, g_low, out_ref):
        @pl.when(lax.axis_index("row") == step + 1)
        def _():
            moved = before_ref[...]
            right = rhs_ref[...] - mm(moved, e_high[...]) - mm(moved, e_low[...])
            out_ref[...] = with_split(right, g_high[...], g_low[...]).astype(BF)

    return pl.pallas_call(
        body,
        in_specs=[vmem()] * 7,
        out_specs=vmem(),
        out_shape=shape(COLS),
        input_output_aliases={0: 0},
        compiler_params=small(4),
    )(sent, rhs, before, *factors)


def pack_body(blocks, tiles, count, slots, coupling_ref, out_ref, place):
    @pl.loop(0, TPR)
    def _(i):
        place[slots[0, i]] = i

    first = lax.axis_index("col") * TPD
    lane = lax.broadcasted_iota(jnp.int32, (TILE, BLK), 1)
    info = jnp.zeros((TILE, BLK), jnp.int32)
    values = []
    for k in range(KCAP):
        info = jnp.where(lane == k, blocks[k], info)
        info = jnp.where(lane == k + TILE, place[first + tiles[k]], info)
        tile = coupling_ref[k].astype(F32)
        values.append(jnp.where(k < count[0], tile, jnp.zeros_like(tile)))
        total = values[k]
        for before in range(k):
            same = (blocks[before] == blocks[k]) & (tiles[before] == tiles[k])
            total = total + jnp.where(same, values[before], jnp.zeros_like(tile))
        out_ref[k] = total.astype(BF)
    out_ref[KCAP] = info.astype(F32).astype(BF)


def pack(coupling, blocks, tiles, count, slots):
    return pl.pallas_call(
        pack_body,
        in_specs=[smem()] * 4 + [vmem()],
        out_specs=vmem(),
        out_shape=jax.ShapeDtypeStruct((KCAP + 1, TILE, BLK), BF),
        scratch_shapes=[pltpu.SMEM((TPR,), jnp.int32)],
        compiler_params=small(2),
        name="pack",
    )(blocks, tiles, count, slots, coupling)


def clear(earlier):
    def body(_, out_ref):
        out_ref[...] = jnp.zeros_like(out_ref)

    return pl.pallas_call(
        body,
        in_specs=[pl.BlockSpec(memory_space=pl.ANY)],
        out_specs=vmem(),
        out_shape=jax.ShapeDtypeStruct((N_ROW, SR, NB), BF),
        compiler_params=small(2),
        name="clear",
    )(earlier)


def build_body(cleared, c0, c1, c2, c3, out_ref, info, codes, sem):
    parts = (c0, c1, c2, c3)
    for part, ref in enumerate(parts):
        for z in range(SIDE):
            info[pl.ds(part * SIDE + z, 1)] = ref[z, KCAP].astype(F32)[:1].astype(jnp.int32)
    move = pltpu.make_async_copy(info, codes, sem)
    move.start()
    move.wait()
    for part, ref in enumerate(parts):

        @pl.loop(0, SIDE)
        def _(z):
            at = part * SIDE + z
            for k in range(KCAP):
                block = codes[at, k]
                row = pl.multiple_of(codes[at, k + TILE] * TILE, TILE)
                lane = pl.multiple_of(block % PER * BLK, BLK)
                out_ref[block // PER, pl.ds(row, TILE), pl.ds(lane, BLK)] = ref[z, k]


def build(parts, cleared):
    return pl.pallas_call(
        build_body,
        in_specs=[vmem()] * 5,
        out_specs=vmem(),
        input_output_aliases={0: 0},
        scratch_shapes=[
            pltpu.VMEM((N_COL, BLK), jnp.int32),
            pltpu.SMEM((N_COL, BLK), jnp.int32),
            pltpu.SemaphoreType.DMA(()),
        ],
        out_shape=jax.ShapeDtypeStruct((N_ROW, SR, NB), BF),
        compiler_params=small(4),
        name="build",
    )(cleared, *parts)


def line_sum(other, c_ref, x_ref):
    row = lax.axis_index("row")
    chip, core = row // 2, row % 2
    side = 1 - core if other else core
    total = None
    for k in range(SIDE):
        group = 2 * ((chip - k) % SIDE) + side
        part = lax.dot_general(c_ref[group], x_ref[k], (((1,), (1,)), ((), ())), preferred_element_type=F32)
        total = part if total is None else total + part
    return total


def own_body(c_ref, x_ref, out_ref):
    out_ref[...] = line_sum(False, c_ref, x_ref)


def other_body(c_ref, x_ref, sum_ref, out_ref):
    out_ref[...] = (sum_ref[...] + line_sum(True, c_ref, x_ref)).T.astype(BF)


def products_own(dense, line):
    return pl.pallas_call(
        own_body,
        in_specs=[vmem()] * 2,
        out_specs=vmem(),
        out_shape=jax.ShapeDtypeStruct((SR, COLS), F32),
        compiler_params=small(4),
        name="products_own",
    )(dense, line)


def products_other(dense, line, sums):
    return pl.pallas_call(
        other_body,
        in_specs=[vmem()] * 3,
        out_specs=vmem(),
        out_shape=jax.ShapeDtypeStruct((COLS, SR), BF),
        compiler_params=small(4),
        name="products_other",
    )(dense, line, sums)


def came_from(dx, dz):
    col = lax.axis_index("col")
    return (col // SIDE - dx) % SIDE * SIDE + (col % SIDE - dz) % SIDE


def final_body(*refs):
    pieces, (s_ref, schur_ref, out_hbm, stacked, turned, out, sems) = refs[:13], refs[13:]
    tall, wide, half = 256, 1024, COLS // 2

    def put(dx, dz, first, value):
        at = pl.multiple_of(came_from(dx, dz) * COLS + first, half)
        stacked[pl.ds(at, value.shape[0]), :] = value

    put(0, 0, 0, pieces[0][...])
    for k in range(1, SIDE):
        put(0, k, 0, pieces[k][...])
        put(k, 0, 0, pieces[3 + k][...])
        for other in range(1, SIDE):
            put(k, other, 0, pieces[6 + k][other - 1])
            put(other, k, half, pieces[9 + k][other - 1])
    moves = []
    for m in range(SR // tall):
        rows = pl.ds(m * tall, tall)
        turned[rows, :] = stacked[:, rows].T
        for n in range(schur_ref.shape[1] // wide):
            cols = pl.ds(n * wide, wide)
            slot = len(moves) % 4
            if len(moves) >= 4:
                moves[-4].wait()
            change = mm(turned[rows, :], s_ref[:, cols])
            out[slot] = (schur_ref[rows, cols].astype(F32) - change).astype(BF)
            moves.append(pltpu.make_async_copy(out.at[slot], out_hbm.at[rows, cols], sems.at[slot]))
            moves[-1].start()
    for move in moves[-4:]:
        move.wait()


def final(pieces, factor, schur):
    return pl.pallas_call(
        final_body,
        in_specs=[vmem()] * 15,
        out_specs=hbm(),
        scratch_shapes=[
            pltpu.VMEM((NRHS, SR), BF),
            pltpu.VMEM((SR, NRHS), BF),
            pltpu.VMEM((4, 256, 1024), BF),
            pltpu.SemaphoreType.DMA((4,)),
        ],
        out_shape=jax.ShapeDtypeStruct(schur.shape, BF),
        compiler_params=small(10),
        name="final",
    )(*pieces, factor, schur)


def turned_cols(value, dx, dz):
    pairs = [(x * SIDE + z, (x + dx) % SIDE * SIDE + (z + dz) % SIDE) for x in range(SIDE) for z in range(SIDE)]
    return lax.ppermute(value, "col", pairs)


def gather_near(value):
    return [value] + [turned_cols(value, 0, dz) for dz in (1, 2, 3)]


def gather_far(near):
    return [near] + [turned_cols(near, dx, 0) for dx in (1, 2, 3)]


def stack_halves(pieces, first):
    half = COLS // 2

    def body(a, b, c, out_ref):
        for at, ref in enumerate((a, b, c)):
            out_ref[at] = ref[first : first + half, :]

    return pl.pallas_call(
        body,
        in_specs=[vmem()] * 3,
        out_specs=vmem(),
        out_shape=jax.ShapeDtypeStruct((SIDE - 1, half, SR), BF),
        compiler_params=small(2),
    )(*pieces)


def gather_cols(value):
    half = COLS // 2
    along_z = [turned_cols(value, 0, k) for k in (1, 2, 3)]
    along_x = [turned_cols(value, k, 0) for k in (1, 2, 3)]
    first = stack_halves(along_z, 0)
    second = stack_halves(along_x, half)
    others = [turned_cols(first, k, 0) for k in (1, 2, 3)] + [turned_cols(second, 0, k) for k in (1, 2, 3)]
    return [value] + along_z + along_x + others


def gather_chips(value, first):
    def moved(k):
        return lax.ppermute(value, "row", [(2 * a + c, 2 * ((a + k) % SIDE) + c) for a in range(SIDE) for c in (0, 1)])

    return jnp.stack([value] + [after(moved(k), first) for k in (1, 2, 3)])


def swap_cores(value):
    return lax.ppermute(value, "row", [(i, i ^ 1) for i in range(N_ROW)])


def after(value, earlier):
    return lax.optimization_barrier((value, earlier))[0]


def shards(rhs, couple_prev, diag_inverse, coupling, pair_block, pair_tile, pair_count, owner_slot, schur, surface_factor):
    sent, *factors = prep(rhs, couple_prev, diag_inverse)
    near = parts = packed = cleared = None
    for step in range(N_ROW - 1):
        before = lax.ppermute(sent, "row", [(step, step + 1)])
        if step == 1:
            packed = pack(after(coupling, sent), pair_block, pair_tile, pair_count, owner_slot)
            before = after(before, packed)
        if step == 2:
            near = gather_near(packed)
        if step == 3:
            before = after(before, near)
        if step == 4:
            near = jnp.stack([near[0]] + [after(part, sent) for part in near[1:]])
            parts = gather_far(near)
            before = after(before, near)
        if step == 5:
            cleared = clear(sent)
            before = after(before, cleared)
        sent = advance(step, sent, before, rhs, factors)
    dense = build([parts[0]] + [after(part, sent) for part in parts[1:]], cleared)
    line = gather_chips(sent, dense)
    other = swap_cores(line)
    update = products_other(dense, other, products_own(dense, line))
    return final(gather_cols(update), surface_factor, schur)


def solution(mesh):
    placed = (
        P("col", "row"),
        P("row", None),
        P("row", None),
        P(("row", "col"), None, None),
        P(("row", "col")),
        P(("row", "col")),
        P(("row", "col")),
        P("row", None),
        P("row", "col"),
        P(None, "col"),
    )

    return jax.shard_map(shards, mesh=mesh, in_specs=placed, out_specs=P("row", "col"), check_vma=False)
```

profile of v0, /device:TPU:0, one launch (start us, length us, event | category | flops | bytes accessed | tf_op | source)
XLA Modules:
  0.0 83.4 jit_solution(7205590724743104224)
XLA Ops:
  0.0 3.9 %prep.1 = (bf16[32,1024]{1,0:T(8,128)(2,1)S(1)}, bf16[1024,1024]{1,0:T(8,128)(2,1)S(1)}, bf16[1024,1024]{1,0:T(8,128)(2,1)S(1)}, bf16[1024,1024]{1,0:T(8,128)(2,1)S(1)}, bf16[1024,1024]{1,0:T(8,128)(2,1)S(1)}) custom-call(f32[32,1024]{1,0:T(8,128)} %rhs_ref.13, f32[1024,1024]{1,0:T(8,128)} %e_hbm.1, f32[1024,1024]{1,0:T(8,128)} %g_hbm.1), custom_call_target="tpu_custom_call" | custom-call | tf_op jit(solution)/shard_map/prep/pallas_call | solution.py:87
  3.9 1.3 %collective-permute-start = (bf16[32,1024]{1,0:T(8,128)(2,1)S(1)}, bf16[32,1024]{1,0:T(8,128)(2,1)S(1)}, u32[]{:S(2)}, u32[]{:S(2)}) collective-permute-start(bf16[32,1024]{1,0:T(8,128)(2,1)S(1)} %get-tuple-element.24.sent_ref), channel_id=1, source_target_pairs={{0,16},{1,17},{2,18},{3,19},{4,20},{5,21},{6,22},{7,23},{8,24},{9,... | collective-permute-start | bytes 196616 | tf_op jit(solution)/shard_map/ppermute | solution.py:360
  5.2 0.9 %collective-permute-done.before_ref = bf16[32,1024]{1,0:T(8,128)(2,1)S(1)} collective-permute-done((bf16[32,1024]{1,0:T(8,128)(2,1)S(1)}, bf16[32,1024]{1,0:T(8,128)(2,1)S(1)}, u32[]{:S(2)}, u32[]{:S(2)}) %collective-permute-start) | collective-permute-done | bytes 65568 | tf_op jit(solution)/shard_map/ppermute | solution.py:360
  6.1 0.8 collective-permute-start.1
  7.6 1.1 %pack.1 = bf16[13,16,128]{2,1,0:T(8,128)(2,1)S(1)} custom-call(s32[12]{0:T(128)S(1)} %copy-done.3, s32[12]{0:T(128)S(1)} %copy-done.4, s32[1]{0:T(128)S(6)} %copy.27.count, s32[1,48]{1,0:T(1,128)S(1)} %copy-done.5, bf16[12,16,128]{2,1,0:T(8,128)(2,1)S(1)} %copy-done.2), custom_call_target="tpu_custom_call" | custom-call | tf_op jit(solution)/shard_map/pack/pallas_call | solution.py:144
  10.2 4.7 %collective-permute-start.6 = (bf16[13,16,128]{2,1,0:T(8,128)(2,1)S(1)}, bf16[13,16,128]{2,1,0:T(8,128)(2,1)S(1)}, u32[]{:S(2)}, u32[]{:S(2)}) collective-permute-start(bf16[13,16,128]{2,1,0:T(8,128)(2,1)S(1)} %pack.1), channel_id=1, source_target_pairs={{0,3},{1,0},{2,1},{3,2},{4,7},{5,4},{6,5},{7,6},{8,11},{9,8},{10,9... | collective-permute-start | bytes 159752 | tf_op jit(solution)/shard_map/ppermute | solution.py:304
  14.9 1.3 %collective-permute-start.4 = (bf16[13,16,128]{2,1,0:T(8,128)(2,1)S(1)}, bf16[13,16,128]{2,1,0:T(8,128)(2,1)S(1)}, u32[]{:S(2)}, u32[]{:S(2)}) collective-permute-start(bf16[13,16,128]{2,1,0:T(8,128)(2,1)S(1)} %pack.1), channel_id=1, source_target_pairs={{0,1},{1,2},{2,3},{3,0},{4,5},{5,6},{6,7},{7,4},{8,9},{9,10},{10,1... | collective-permute-start | bytes 159752 | tf_op jit(solution)/shard_map/ppermute | solution.py:304
  16.6 3.9 %collective-permute-done.5 = bf16[13,16,128]{2,1,0:T(8,128)(2,1)S(1)} collective-permute-done((bf16[13,16,128]{2,1,0:T(8,128)(2,1)S(1)}, bf16[13,16,128]{2,1,0:T(8,128)(2,1)S(1)}, u32[]{:S(2)}, u32[]{:S(2)}) %collective-permute-start.5) | collective-permute-done | bytes 53280 | tf_op jit(solution)/shard_map/ppermute | solution.py:304
  20.8 2.8 %collective-permute-start.12 = (bf16[4,13,16,128]{3,2,1,0:T(8,128)(2,1)S(1)}, bf16[4,13,16,128]{3,2,1,0:T(8,128)(2,1)S(1)}, u32[]{:S(2)}, u32[]{:S(2)}) collective-permute-start(bf16[4,13,16,128]{3,2,1,0:T(8,128)(2,1)S(1)} %pad_maximum_fusion.1.c0), channel_id=1, source_target_pairs={{0,12},{1,13},{2,14},{3,15},{4,0},{5,1},{6,2},{7,3},{8,4},{9,5},{1... | collective-permute-start | bytes 638984 | tf_op jit(solution)/shard_map/ppermute | solution.py:304
  24.3 0.9 %collective-permute-start.11 = (bf16[4,13,16,128]{3,2,1,0:T(8,128)(2,1)S(1)}, bf16[4,13,16,128]{3,2,1,0:T(8,128)(2,1)S(1)}, u32[]{:S(2)}, u32[]{:S(2)}) collective-permute-start(bf16[4,13,16,128]{3,2,1,0:T(8,128)(2,1)S(1)} %pad_maximum_fusion.1.c0), channel_id=1, source_target_pairs={{0,8},{1,9},{2,10},{3,11},{4,12},{5,13},{6,14},{7,15},{8,0},{9,1},... | collective-permute-start | bytes 638984 | tf_op jit(solution)/shard_map/ppermute | solution.py:304
  25.2 0.9 %collective-permute-start.8 = (bf16[4,13,16,128]{3,2,1,0:T(8,128)(2,1)S(1)}, bf16[4,13,16,128]{3,2,1,0:T(8,128)(2,1)S(1)}, u32[]{:S(2)}, u32[]{:S(2)}) collective-permute-start(bf16[4,13,16,128]{3,2,1,0:T(8,128)(2,1)S(1)} %pad_maximum_fusion.1.c0), channel_id=1, source_target_pairs={{0,4},{1,5},{2,6},{3,7},{4,8},{5,9},{6,10},{7,11},{8,12},{9,13},{1... | collective-permute-start | bytes 638984 | tf_op jit(solution)/shard_map/ppermute | solution.py:304
  26.7 0.8 clear.1.cleared
  28.5 11.1 %collective-permute-start.15 = (bf16[32,1024]{1,0:T(8,128)(2,1)S(1)}, bf16[32,1024]{1,0:T(8,128)(2,1)S(1)}, u32[]{:S(2)}, u32[]{:S(2)}) collective-permute-start(bf16[32,1024]{1,0:T(8,128)(2,1)S(1)} %shard_map.106), channel_id=1, source_target_pairs={{0,96},{16,112},{32,0},{48,16},{64,32},{80,48},{96,64},{112,80},{1... | collective-permute-start | bytes 196616 | tf_op jit(solution)/shard_map/ppermute | solution.py:343
  39.6 1.1 %collective-permute-start.13 = (bf16[32,1024]{1,0:T(8,128)(2,1)S(1)}, bf16[32,1024]{1,0:T(8,128)(2,1)S(1)}, u32[]{:S(2)}, u32[]{:S(2)}) collective-permute-start(bf16[32,1024]{1,0:T(8,128)(2,1)S(1)} %shard_map.106), channel_id=1, source_target_pairs={{0,32},{16,48},{32,64},{48,80},{64,96},{80,112},{96,0},{112,16},{1... | collective-permute-start | bytes 196616 | tf_op jit(solution)/shard_map/ppermute | solution.py:343
  40.6 2.3 %build.1.c_ref = bf16[8,768,1024]{2,1,0:T(8,128)(2,1)S(1)} custom-call(bf16[8,768,1024]{2,1,0:T(8,128)(2,1)S(1)} %clear.1.cleared, bf16[4,13,16,128]{3,2,1,0:T(8,128)(2,1)S(1)} %pad_maximum_fusion.1.c0, bf16[4,13,16,128]{3,2,1,0:T(8,128)(2,1)S(1)} %collective-permute-done.8.c1, ...), custom_call_target="tpu_custom_call", output_to_operand_aliasing={{}: (0, {})} | custom-call | tf_op jit(solution)/shard_map/build/pallas_call | solution.py:190
  43.0 2.5 %collective-permute-done.14 = bf16[32,1024]{1,0:T(8,128)(2,1)S(1)} collective-permute-done((bf16[32,1024]{1,0:T(8,128)(2,1)S(1)}, bf16[32,1024]{1,0:T(8,128)(2,1)S(1)}, u32[]{:S(2)}, u32[]{:S(2)}) %collective-permute-start.14) | collective-permute-done | bytes 65568 | tf_op jit(solution)/shard_map/ppermute | solution.py:343
  45.5 1.3 %collective-permute-done.13 = bf16[32,1024]{1,0:T(8,128)(2,1)S(1)} collective-permute-done((bf16[32,1024]{1,0:T(8,128)(2,1)S(1)}, bf16[32,1024]{1,0:T(8,128)(2,1)S(1)}, u32[]{:S(2)}, u32[]{:S(2)}) %collective-permute-start.13) | collective-permute-done | bytes 65568 | tf_op jit(solution)/shard_map/ppermute | solution.py:343
  47.1 1.8 %products_own.1.sum_ref = f32[768,32]{1,0:T(8,128)S(1)} custom-call(bf16[8,768,1024]{2,1,0:T(8,128)(2,1)S(1)} %build.1.c_ref, bf16[4,32,1024]{2,1,0:T(8,128)(2,1)S(1)} %pad_maximum_fusion.x_ref), custom_call_target="tpu_custom_call" | custom-call | tf_op jit(solution)/shard_map/products_own/pallas_call | solution.py:227
  48.9 1.8 %products_other.1.refs_0_ = bf16[32,768]{1,0:T(8,128)(2,1)S(1)} custom-call(bf16[8,768,1024]{2,1,0:T(8,128)(2,1)S(1)} %build.1.c_ref, bf16[4,32,1024]{2,1,0:T(8,128)(2,1)S(1)} %collective-permute-done.16.x_ref, f32[768,32]{1,0:T(8,128)S(1)} %products_own.1.sum_ref), custom_call_target="tpu_custom_call" | custom-call | tf_op jit(solution)/shard_map/products_other/pallas_call | solution.py:238
  50.8 0.9 %collective-permute-start.22 = (bf16[32,768]{1,0:T(8,128)(2,1)S(1)}, bf16[32,768]{1,0:T(8,128)(2,1)S(1)}, u32[]{:S(2)}, u32[]{:S(2)}) collective-permute-start(bf16[32,768]{1,0:T(8,128)(2,1)S(1)} %products_other.1.refs_0_), channel_id=1, source_target_pairs={{0,12},{1,13},{2,14},{3,15},{4,0},{5,1},{6,2},{7,3},{8,4},{9,5},{1... | collective-permute-start | bytes 147464 | tf_op jit(solution)/shard_map/ppermute | solution.py:304
  52.1 0.9 %collective-permute-start.20 = (bf16[32,768]{1,0:T(8,128)(2,1)S(1)}, bf16[32,768]{1,0:T(8,128)(2,1)S(1)}, u32[]{:S(2)}, u32[]{:S(2)}) collective-permute-start(bf16[32,768]{1,0:T(8,128)(2,1)S(1)} %products_other.1.refs_0_), channel_id=1, source_target_pairs={{0,4},{1,5},{2,6},{3,7},{4,8},{5,9},{6,10},{7,11},{8,12},{9,13},{1... | collective-permute-start | bytes 147464 | tf_op jit(solution)/shard_map/ppermute | solution.py:304
  53.0 2.3 %collective-permute-done.22.c.refs_6_ = bf16[32,768]{1,0:T(8,128)(2,1)S(1)} collective-permute-done((bf16[32,768]{1,0:T(8,128)(2,1)S(1)}, bf16[32,768]{1,0:T(8,128)(2,1)S(1)}, u32[]{:S(2)}, u32[]{:S(2)}) %collective-permute-start.22) | collective-permute-done | bytes 49184 | tf_op jit(solution)/shard_map/ppermute | solution.py:304
  55.3 2.0 %collective-permute-done.21.b.refs_5_ = bf16[32,768]{1,0:T(8,128)(2,1)S(1)} collective-permute-done((bf16[32,768]{1,0:T(8,128)(2,1)S(1)}, bf16[32,768]{1,0:T(8,128)(2,1)S(1)}, u32[]{:S(2)}, u32[]{:S(2)}) %collective-permute-start.21) | collective-permute-done | bytes 49184 | tf_op jit(solution)/shard_map/ppermute | solution.py:304
  57.9 4.0 %collective-permute-start.28 = (bf16[3,16,768]{2,1,0:T(8,128)(2,1)S(1)}, bf16[3,16,768]{2,1,0:T(8,128)(2,1)S(1)}, u32[]{:S(2)}, u32[]{:S(2)}) collective-permute-start(bf16[3,16,768]{2,1,0:T(8,128)(2,1)S(1)} %shard_map.108), channel_id=1, source_target_pairs={{0,3},{1,0},{2,1},{3,2},{4,7},{5,4},{6,5},{7,6},{8,11},{9,8},{10,9... | collective-permute-start | bytes 221192 | tf_op jit(solution)/shard_map/ppermute | solution.py:304
  62.3 1.6 %collective-permute-start.17 = (bf16[32,768]{1,0:T(8,128)(2,1)S(1)}, bf16[32,768]{1,0:T(8,128)(2,1)S(1)}, u32[]{:S(2)}, u32[]{:S(2)}) collective-permute-start(bf16[32,768]{1,0:T(8,128)(2,1)S(1)} %products_other.1.refs_0_), channel_id=1, source_target_pairs={{0,1},{1,2},{2,3},{3,0},{4,5},{5,6},{6,7},{7,4},{8,9},{9,10},{10,1... | collective-permute-start | bytes 147464 | tf_op jit(solution)/shard_map/ppermute | solution.py:304
  63.9 4.1 %collective-permute-start.27 = (bf16[3,16,768]{2,1,0:T(8,128)(2,1)S(1)}, bf16[3,16,768]{2,1,0:T(8,128)(2,1)S(1)}, u32[]{:S(2)}, u32[]{:S(2)}) collective-permute-start(bf16[3,16,768]{2,1,0:T(8,128)(2,1)S(1)} %shard_map.108), channel_id=1, source_target_pairs={{0,2},{1,3},{2,0},{3,1},{4,6},{5,7},{6,4},{7,5},{8,10},{9,11},{10,... | collective-permute-start | bytes 221192 | tf_op jit(solution)/shard_map/ppermute | solution.py:304
  68.3 1.2 %collective-permute-done.17.a.refs_1_ = bf16[32,768]{1,0:T(8,128)(2,1)S(1)} collective-permute-done((bf16[32,768]{1,0:T(8,128)(2,1)S(1)}, bf16[32,768]{1,0:T(8,128)(2,1)S(1)}, u32[]{:S(2)}, u32[]{:S(2)}) %collective-permute-start.17) | collective-permute-done | bytes 49184 | tf_op jit(solution)/shard_map/ppermute | solution.py:304
  69.6 1.2 %collective-permute-start.25 = (bf16[3,16,768]{2,1,0:T(8,128)(2,1)S(1)}, bf16[3,16,768]{2,1,0:T(8,128)(2,1)S(1)}, u32[]{:S(2)}, u32[]{:S(2)}) collective-permute-start(bf16[3,16,768]{2,1,0:T(8,128)(2,1)S(1)} %shard_map.107), channel_id=1, source_target_pairs={{0,12},{1,13},{2,14},{3,15},{4,0},{5,1},{6,2},{7,3},{8,4},{9,5},{1... | collective-permute-start | bytes 221192 | tf_op jit(solution)/shard_map/ppermute | solution.py:304
  70.8 1.0 %collective-permute-start.24 = (bf16[3,16,768]{2,1,0:T(8,128)(2,1)S(1)}, bf16[3,16,768]{2,1,0:T(8,128)(2,1)S(1)}, u32[]{:S(2)}, u32[]{:S(2)}) collective-permute-start(bf16[3,16,768]{2,1,0:T(8,128)(2,1)S(1)} %shard_map.107), channel_id=1, source_target_pairs={{0,8},{1,9},{2,10},{3,11},{4,12},{5,13},{6,14},{7,15},{8,0},{9,1},... | collective-permute-start | bytes 221192 | tf_op jit(solution)/shard_map/ppermute | solution.py:304
  72.0 1.7 %collective-permute-done.26.refs_10_ = bf16[3,16,768]{2,1,0:T(8,128)(2,1)S(1)} collective-permute-done((bf16[3,16,768]{2,1,0:T(8,128)(2,1)S(1)}, bf16[3,16,768]{2,1,0:T(8,128)(2,1)S(1)}, u32[]{:S(2)}, u32[]{:S(2)}) %collective-permute-start.26) | collective-permute-done | bytes 73760 | tf_op jit(solution)/shard_map/ppermute | solution.py:304
  73.9 2.7 %collective-permute-done.24.refs_8_ = bf16[3,16,768]{2,1,0:T(8,128)(2,1)S(1)} collective-permute-done((bf16[3,16,768]{2,1,0:T(8,128)(2,1)S(1)}, bf16[3,16,768]{2,1,0:T(8,128)(2,1)S(1)}, u32[]{:S(2)}, u32[]{:S(2)}) %collective-permute-start.24) | collective-permute-done | bytes 73760 | tf_op jit(solution)/shard_map/ppermute | solution.py:304
  77.4 5.8 %final.1 = bf16[768,4096]{1,0:T(8,128)(2,1)} custom-call(bf16[32,768]{1,0:T(8,128)(2,1)S(1)} %products_other.1.refs_0_, bf16[32,768]{1,0:T(8,128)(2,1)S(1)} %collective-permute-done.17.a.refs_1_, bf16[32,768]{1,0:T(8,128)(2,1)S(1)} %collective-permute-done.18.b.refs_2_, bf16[32,768]{1,0:T(8,128)(2,1)S(1)} %collective-permute-done.19.c.refs_3_, ...), custom_call_target="tpu_custom_call" | custom-call | tf_op jit(solution)/shard_map/final/pallas_call | solution.py:286
  (61 shorter events, 7.8 us)
Async XLA Ops:
  3.9 2.2 %collective-permute-start = (bf16[32,1024]{1,0:T(8,128)(2,1)S(1)}, bf16[32,1024]{1,0:T(8,128)(2,1)S(1)}, u32[]{:S(2)}, u32[]{:S(2)}) collective-permute-start(bf16[32,1024]{1,0:T(8,128)(2,1)S(1)} %get-tuple-element.24.sent_ref), channel_id=1, source_target_pairs={{0,16},{1,17},{2,18},{3,19},{4,20},{5,21},{6,22},{7,23},{8,24},{9,... | collective-permute-start | bytes 196616 | tf_op jit(solution)/shard_map/ppermute | solution.py:360
  6.1 2.6 %collective-permute-start.1 = (bf16[32,1024]{1,0:T(8,128)(2,1)S(1)}, bf16[32,1024]{1,0:T(8,128)(2,1)S(1)}, u32[]{:S(2)}, u32[]{:S(2)}) collective-permute-start(bf16[32,1024]{1,0:T(8,128)(2,1)S(1)} %shard_map.100.sent_ref), channel_id=1, source_target_pairs={{16,32},{17,33},{18,34},{19,35},{20,36},{21,37},{22,38},{23,39},{2... | collective-permute-start | bytes 196616 | tf_op jit(solution)/shard_map/ppermute | solution.py:360
  8.8 0.7 collective-permute-start.2
  9.5 11.3 %collective-permute-start.3 = (bf16[32,1024]{1,0:T(8,128)(2,1)S(1)}, bf16[32,1024]{1,0:T(8,128)(2,1)S(1)}, u32[]{:S(2)}, u32[]{:S(2)}) collective-permute-start(bf16[32,1024]{1,0:T(8,128)(2,1)S(1)} %shard_map.102.sent_ref), channel_id=1, source_target_pairs={{48,64},{49,65},{50,66},{51,67},{52,68},{53,69},{54,70},{55,71},{5... | collective-permute-start | bytes 196616 | tf_op jit(solution)/shard_map/ppermute | solution.py:360
  10.2 6.5 %collective-permute-start.6 = (bf16[13,16,128]{2,1,0:T(8,128)(2,1)S(1)}, bf16[13,16,128]{2,1,0:T(8,128)(2,1)S(1)}, u32[]{:S(2)}, u32[]{:S(2)}) collective-permute-start(bf16[13,16,128]{2,1,0:T(8,128)(2,1)S(1)} %pack.1), channel_id=1, source_target_pairs={{0,3},{1,0},{2,1},{3,2},{4,7},{5,4},{6,5},{7,6},{8,11},{9,8},{10,9... | collective-permute-start | bytes 159752 | tf_op jit(solution)/shard_map/ppermute | solution.py:304
  14.8 5.7 %collective-permute-start.5 = (bf16[13,16,128]{2,1,0:T(8,128)(2,1)S(1)}, bf16[13,16,128]{2,1,0:T(8,128)(2,1)S(1)}, u32[]{:S(2)}, u32[]{:S(2)}) collective-permute-start(bf16[13,16,128]{2,1,0:T(8,128)(2,1)S(1)} %pack.1), channel_id=1, source_target_pairs={{0,2},{1,3},{2,0},{3,1},{4,6},{5,7},{6,4},{7,5},{8,10},{9,11},{10,... | collective-permute-start | bytes 159752 | tf_op jit(solution)/shard_map/ppermute | solution.py:304
  14.9 5.9 %collective-permute-start.4 = (bf16[13,16,128]{2,1,0:T(8,128)(2,1)S(1)}, bf16[13,16,128]{2,1,0:T(8,128)(2,1)S(1)}, u32[]{:S(2)}, u32[]{:S(2)}) collective-permute-start(bf16[13,16,128]{2,1,0:T(8,128)(2,1)S(1)} %pack.1), channel_id=1, source_target_pairs={{0,1},{1,2},{2,3},{3,0},{4,5},{5,6},{6,7},{7,4},{8,9},{9,10},{10,1... | collective-permute-start | bytes 159752 | tf_op jit(solution)/shard_map/ppermute | solution.py:304
  20.8 18.8 %collective-permute-start.12 = (bf16[4,13,16,128]{3,2,1,0:T(8,128)(2,1)S(1)}, bf16[4,13,16,128]{3,2,1,0:T(8,128)(2,1)S(1)}, u32[]{:S(2)}, u32[]{:S(2)}) collective-permute-start(bf16[4,13,16,128]{3,2,1,0:T(8,128)(2,1)S(1)} %pad_maximum_fusion.1.c0), channel_id=1, source_target_pairs={{0,12},{1,13},{2,14},{3,15},{4,0},{5,1},{6,2},{7,3},{8,4},{9,5},{1... | collective-permute-start | bytes 638984 | tf_op jit(solution)/shard_map/ppermute | solution.py:304
  23.6 2.4 %collective-permute-start.7 = (bf16[32,1024]{1,0:T(8,128)(2,1)S(1)}, bf16[32,1024]{1,0:T(8,128)(2,1)S(1)}, u32[]{:S(2)}, u32[]{:S(2)}) collective-permute-start(bf16[32,1024]{1,0:T(8,128)(2,1)S(1)} %shard_map.103.sent_ref), channel_id=1, source_target_pairs={{64,80},{65,81},{66,82},{67,83},{68,84},{69,85},{70,86},{71,87},{7... | collective-permute-start | bytes 196616 | tf_op jit(solution)/shard_map/ppermute | solution.py:360
  24.3 16.3 %collective-permute-start.11 = (bf16[4,13,16,128]{3,2,1,0:T(8,128)(2,1)S(1)}, bf16[4,13,16,128]{3,2,1,0:T(8,128)(2,1)S(1)}, u32[]{:S(2)}, u32[]{:S(2)}) collective-permute-start(bf16[4,13,16,128]{3,2,1,0:T(8,128)(2,1)S(1)} %pad_maximum_fusion.1.c0), channel_id=1, source_target_pairs={{0,8},{1,9},{2,10},{3,11},{4,12},{5,13},{6,14},{7,15},{8,0},{9,1},... | collective-permute-start | bytes 638984 | tf_op jit(solution)/shard_map/ppermute | solution.py:304
  25.2 15.5 %collective-permute-start.8 = (bf16[4,13,16,128]{3,2,1,0:T(8,128)(2,1)S(1)}, bf16[4,13,16,128]{3,2,1,0:T(8,128)(2,1)S(1)}, u32[]{:S(2)}, u32[]{:S(2)}) collective-permute-start(bf16[4,13,16,128]{3,2,1,0:T(8,128)(2,1)S(1)} %pad_maximum_fusion.1.c0), channel_id=1, source_target_pairs={{0,4},{1,5},{2,6},{3,7},{4,8},{5,9},{6,10},{7,11},{8,12},{9,13},{1... | collective-permute-start | bytes 638984 | tf_op jit(solution)/shard_map/ppermute | solution.py:304
  26.1 1.5 %collective-permute-start.9 = (bf16[32,1024]{1,0:T(8,128)(2,1)S(1)}, bf16[32,1024]{1,0:T(8,128)(2,1)S(1)}, u32[]{:S(2)}, u32[]{:S(2)}) collective-permute-start(bf16[32,1024]{1,0:T(8,128)(2,1)S(1)} %shard_map.104._.sent_ref), channel_id=1, source_target_pairs={{80,96},{81,97},{82,98},{83,99},{84,100},{85,101},{86,102},{87,103... | collective-permute-start | bytes 196616 | tf_op jit(solution)/shard_map/ppermute | solution.py:360
  27.6 0.7 collective-permute-start.10
  28.5 14.5 %collective-permute-start.15 = (bf16[32,1024]{1,0:T(8,128)(2,1)S(1)}, bf16[32,1024]{1,0:T(8,128)(2,1)S(1)}, u32[]{:S(2)}, u32[]{:S(2)}) collective-permute-start(bf16[32,1024]{1,0:T(8,128)(2,1)S(1)} %shard_map.106), channel_id=1, source_target_pairs={{0,96},{16,112},{32,0},{48,16},{64,32},{80,48},{96,64},{112,80},{1... | collective-permute-start | bytes 196616 | tf_op jit(solution)/shard_map/ppermute | solution.py:343
  39.6 5.9 %collective-permute-start.14 = (bf16[32,1024]{1,0:T(8,128)(2,1)S(1)}, bf16[32,1024]{1,0:T(8,128)(2,1)S(1)}, u32[]{:S(2)}, u32[]{:S(2)}) collective-permute-start(bf16[32,1024]{1,0:T(8,128)(2,1)S(1)} %shard_map.106), channel_id=1, source_target_pairs={{0,64},{16,80},{32,96},{48,112},{64,0},{80,16},{96,32},{112,48},{1... | collective-permute-start | bytes 196616 | tf_op jit(solution)/shard_map/ppermute | solution.py:343
  39.6 7.2 %collective-permute-start.13 = (bf16[32,1024]{1,0:T(8,128)(2,1)S(1)}, bf16[32,1024]{1,0:T(8,128)(2,1)S(1)}, u32[]{:S(2)}, u32[]{:S(2)}) collective-permute-start(bf16[32,1024]{1,0:T(8,128)(2,1)S(1)} %shard_map.106), channel_id=1, source_target_pairs={{0,32},{16,48},{32,64},{48,80},{64,96},{80,112},{96,0},{112,16},{1... | collective-permute-start | bytes 196616 | tf_op jit(solution)/shard_map/ppermute | solution.py:343
  46.8 2.1 %collective-permute-start.16 = (bf16[4,32,1024]{2,1,0:T(8,128)(2,1)S(1)}, bf16[4,32,1024]{2,1,0:T(8,128)(2,1)S(1)}, u32[]{:S(2)}, u32[]{:S(2)}) collective-permute-start(bf16[4,32,1024]{2,1,0:T(8,128)(2,1)S(1)} %pad_maximum_fusion.x_ref), channel_id=1, source_target_pairs={{0,16},{16,0},{32,48},{48,32},{64,80},{80,64},{96,112},{112,96},{1... | collective-permute-start | bytes 786440 | tf_op jit(solution)/shard_map/ppermute | solution.py:349
  47.1 30.3 %slice-start = ((s8[6291456]{0:T(1024)(128)(4,1)}), s8[4194304]{0:T(1024)(128)(4,1)S(1)}, s32[]{:S(2)}) async-start(s8[6291456]{0:T(1024)(128)(4,1)} %bitcast.8), calls=%async_computation | async-start | bytes 8388608
  48.9 28.6 %slice-start.1 = ((s8[6291456]{0:T(1024)(128)(4,1)}), s8[2097152]{0:T(1024)(128)(4,1)S(1)}, s32[]{:S(2)}) async-start(s8[6291456]{0:T(1024)(128)(4,1)} %bitcast.8), calls=%async_computation.1 | async-start | bytes 4194304
  48.9 28.5 %copy-start.1 = (bf16[512,4096]{1,0:T(8,128)(2,1)S(1)}, bf16[512,4096]{1,0:T(8,128)(2,1)}, u32[]{:S(2)}) copy-start(bf16[512,4096]{1,0:T(8,128)(2,1)} %refs_13_.1) | copy-start | bytes 12582916
  50.8 4.5 %collective-permute-start.22 = (bf16[32,768]{1,0:T(8,128)(2,1)S(1)}, bf16[32,768]{1,0:T(8,128)(2,1)S(1)}, u32[]{:S(2)}, u32[]{:S(2)}) collective-permute-start(bf16[32,768]{1,0:T(8,128)(2,1)S(1)} %products_other.1.refs_0_), channel_id=1, source_target_pairs={{0,12},{1,13},{2,14},{3,15},{4,0},{5,1},{6,2},{7,3},{8,4},{9,5},{1... | collective-permute-start | bytes 147464 | tf_op jit(solution)/shard_map/ppermute | solution.py:304
  51.6 5.6 %collective-permute-start.21 = (bf16[32,768]{1,0:T(8,128)(2,1)S(1)}, bf16[32,768]{1,0:T(8,128)(2,1)S(1)}, u32[]{:S(2)}, u32[]{:S(2)}) collective-permute-start(bf16[32,768]{1,0:T(8,128)(2,1)S(1)} %products_other.1.refs_0_), channel_id=1, source_target_pairs={{0,8},{1,9},{2,10},{3,11},{4,12},{5,13},{6,14},{7,15},{8,0},{9,1},... | collective-permute-start | bytes 147464 | tf_op jit(solution)/shard_map/ppermute | solution.py:304
  52.1 5.7 %collective-permute-start.20 = (bf16[32,768]{1,0:T(8,128)(2,1)S(1)}, bf16[32,768]{1,0:T(8,128)(2,1)S(1)}, u32[]{:S(2)}, u32[]{:S(2)}) collective-permute-start(bf16[32,768]{1,0:T(8,128)(2,1)S(1)} %products_other.1.refs_0_), channel_id=1, source_target_pairs={{0,4},{1,5},{2,6},{3,7},{4,8},{5,9},{6,10},{7,11},{8,12},{9,13},{1... | collective-permute-start | bytes 147464 | tf_op jit(solution)/shard_map/ppermute | solution.py:304
  57.9 13.9 %collective-permute-start.28 = (bf16[3,16,768]{2,1,0:T(8,128)(2,1)S(1)}, bf16[3,16,768]{2,1,0:T(8,128)(2,1)S(1)}, u32[]{:S(2)}, u32[]{:S(2)}) collective-permute-start(bf16[3,16,768]{2,1,0:T(8,128)(2,1)S(1)} %shard_map.108), channel_id=1, source_target_pairs={{0,3},{1,0},{2,1},{3,2},{4,7},{5,4},{6,5},{7,6},{8,11},{9,8},{10,9... | collective-permute-start | bytes 221192 | tf_op jit(solution)/shard_map/ppermute | solution.py:304
  61.9 6.2 %collective-permute-start.19 = (bf16[32,768]{1,0:T(8,128)(2,1)S(1)}, bf16[32,768]{1,0:T(8,128)(2,1)S(1)}, u32[]{:S(2)}, u32[]{:S(2)}) collective-permute-start(bf16[32,768]{1,0:T(8,128)(2,1)S(1)} %products_other.1.refs_0_), channel_id=1, source_target_pairs={{0,3},{1,0},{2,1},{3,2},{4,7},{5,4},{6,5},{7,6},{8,11},{9,8},{10,9... | collective-permute-start | bytes 147464 | tf_op jit(solution)/shard_map/ppermute | solution.py:304
  62.3 6.0 %collective-permute-start.18 = (bf16[32,768]{1,0:T(8,128)(2,1)S(1)}, bf16[32,768]{1,0:T(8,128)(2,1)S(1)}, u32[]{:S(2)}, u32[]{:S(2)}) collective-permute-start(bf16[32,768]{1,0:T(8,128)(2,1)S(1)} %products_other.1.refs_0_), channel_id=1, source_target_pairs={{0,2},{1,3},{2,0},{3,1},{4,6},{5,7},{6,4},{7,5},{8,10},{9,11},{10,... | collective-permute-start | bytes 147464 | tf_op jit(solution)/shard_map/ppermute | solution.py:304
  62.3 7.2 %collective-permute-start.17 = (bf16[32,768]{1,0:T(8,128)(2,1)S(1)}, bf16[32,768]{1,0:T(8,128)(2,1)S(1)}, u32[]{:S(2)}, u32[]{:S(2)}) collective-permute-start(bf16[32,768]{1,0:T(8,128)(2,1)S(1)} %products_other.1.refs_0_), channel_id=1, source_target_pairs={{0,1},{1,2},{2,3},{3,0},{4,5},{5,6},{6,7},{7,4},{8,9},{9,10},{10,1... | collective-permute-start | bytes 147464 | tf_op jit(solution)/shard_map/ppermute | solution.py:304
  63.9 8.0 %collective-permute-start.27 = (bf16[3,16,768]{2,1,0:T(8,128)(2,1)S(1)}, bf16[3,16,768]{2,1,0:T(8,128)(2,1)S(1)}, u32[]{:S(2)}, u32[]{:S(2)}) collective-permute-start(bf16[3,16,768]{2,1,0:T(8,128)(2,1)S(1)} %shard_map.108), channel_id=1, source_target_pairs={{0,2},{1,3},{2,0},{3,1},{4,6},{5,7},{6,4},{7,5},{8,10},{9,11},{10,... | collective-permute-start | bytes 221192 | tf_op jit(solution)/shard_map/ppermute | solution.py:304
  68.1 5.6 %collective-permute-start.26 = (bf16[3,16,768]{2,1,0:T(8,128)(2,1)S(1)}, bf16[3,16,768]{2,1,0:T(8,128)(2,1)S(1)}, u32[]{:S(2)}, u32[]{:S(2)}) collective-permute-start(bf16[3,16,768]{2,1,0:T(8,128)(2,1)S(1)} %shard_map.108), channel_id=1, source_target_pairs={{0,1},{1,2},{2,3},{3,0},{4,5},{5,6},{6,7},{7,4},{8,9},{9,10},{10,1... | collective-permute-start | bytes 221192 | tf_op jit(solution)/shard_map/ppermute | solution.py:304
  69.6 4.4 %collective-permute-start.25 = (bf16[3,16,768]{2,1,0:T(8,128)(2,1)S(1)}, bf16[3,16,768]{2,1,0:T(8,128)(2,1)S(1)}, u32[]{:S(2)}, u32[]{:S(2)}) collective-permute-start(bf16[3,16,768]{2,1,0:T(8,128)(2,1)S(1)} %shard_map.107), channel_id=1, source_target_pairs={{0,12},{1,13},{2,14},{3,15},{4,0},{5,1},{6,2},{7,3},{8,4},{9,5},{1... | collective-permute-start | bytes 221192 | tf_op jit(solution)/shard_map/ppermute | solution.py:304
  70.8 5.9 %collective-permute-start.24 = (bf16[3,16,768]{2,1,0:T(8,128)(2,1)S(1)}, bf16[3,16,768]{2,1,0:T(8,128)(2,1)S(1)}, u32[]{:S(2)}, u32[]{:S(2)}) collective-permute-start(bf16[3,16,768]{2,1,0:T(8,128)(2,1)S(1)} %shard_map.107), channel_id=1, source_target_pairs={{0,8},{1,9},{2,10},{3,11},{4,12},{5,13},{6,14},{7,15},{8,0},{9,1},... | collective-permute-start | bytes 221192 | tf_op jit(solution)/shard_map/ppermute | solution.py:304
  71.7 5.7 %collective-permute-start.23 = (bf16[3,16,768]{2,1,0:T(8,128)(2,1)S(1)}, bf16[3,16,768]{2,1,0:T(8,128)(2,1)S(1)}, u32[]{:S(2)}, u32[]{:S(2)}) collective-permute-start(bf16[3,16,768]{2,1,0:T(8,128)(2,1)S(1)} %shard_map.107), channel_id=1, source_target_pairs={{0,4},{1,5},{2,6},{3,7},{4,8},{5,9},{6,10},{7,11},{8,12},{9,13},{1... | collective-permute-start | bytes 221192 | tf_op jit(solution)/shard_map/ppermute | solution.py:304
  (5 other events, 12.1 us)
where the time goes:
time: 83.6 us; the launch traced here: 83.4 us
  starting transfers between devices  43.2 us (52%)
  waiting for transfers between devices  21.1 us (25%)
  Pallas kernels  17.8 us (21%)
  between operations  1.11 us (1%)
    ppermute x18, starting transfers between devices, turned_cols(): return lax.ppermute(value, 'col', pairs)  25.4 us
    ppermute x18, waiting for transfers between devices, turned_cols(): return lax.ppermute(value, 'col', pairs)  16.5 us
    ppermute x3, starting transfers between devices, moved(): lax.ppermute(value, 'row', [(2 * a + c, 2 * ((a + k) % SIDE) + c) for a i...  12.2 us
    pallas_call x1, Pallas kernels, final(): pl.pallas_call(final_body, in_specs=[vmem()] * 15, out_specs=hbm(), scrat...  5.76 us
    ppermute x7, starting transfers between devices, shards(): before = lax.ppermute(sent, 'row', [(step, step + 1)])  5.39 us
    pallas_call x1, Pallas kernels, prep(): pl.pallas_call(prep_body, in_specs=[hbm()] * 3, out_specs=[vmem()] * 5, o...  3.89 us
    ppermute x3, waiting for transfers between devices, moved(): lax.ppermute(value, 'row', [(2 * a + c, 2 * ((a + k) % SIDE) + c) for a i...  3.77 us
    pallas_call x1, Pallas kernels, build(): pl.pallas_call(build_body, in_specs=[vmem()] * 5, out_specs=vmem(), input...  2.33 us
  transfers between devices with their start and end apart: 29, of which 15 were waited for; matrix products, arithmetic and copies ran while one was open for 0% of the time, Pallas kernels for 8%

commit v1 on v0

--- a/solution.py
+++ b/solution.py
@@ -19,6 +19,7 @@
 PER = NB // BLK
 SIDE = 4
 CHUNKS = 4
+WIDE = 512
 BF = jnp.bfloat16
 F32 = jnp.float32
 
@@ -245,58 +246,64 @@
     )(dense, line, sums)
 
 
-def came_from(dx, dz):
+def change_blocks(parts, shifts, s_ref, stacked, turned):
     col = lax.axis_index("col")
-    return (col // SIDE - dx) % SIDE * SIDE + (col % SIDE - dz) % SIDE
-
-
-def final_body(*refs):
-    pieces, (s_ref, schur_ref, out_hbm, stacked, turned, out, sems) = refs[:13], refs[13:]
-    tall, wide, half = 256, 1024, COLS // 2
-
-    def put(dx, dz, first, value):
-        at = pl.multiple_of(came_from(dx, dz) * COLS + first, half)
-        stacked[pl.ds(at, value.shape[0]), :] = value
-
-    put(0, 0, 0, pieces[0][...])
-    for k in range(1, SIDE):
-        put(0, k, 0, pieces[k][...])
-        put(k, 0, 0, pieces[3 + k][...])
-        for other in range(1, SIDE):
-            put(k, other, 0, pieces[6 + k][other - 1])
-            put(other, k, half, pieces[9 + k][other - 1])
-    moves = []
-    for m in range(SR // tall):
-        rows = pl.ds(m * tall, tall)
-        turned[rows, :] = stacked[:, rows].T
-        for n in range(schur_ref.shape[1] // wide):
-            cols = pl.ds(n * wide, wide)
-            slot = len(moves) % 4
-            if len(moves) >= 4:
-                moves[-4].wait()
-            change = mm(turned[rows, :], s_ref[:, cols])
-            out[slot] = (schur_ref[rows, cols].astype(F32) - change).astype(BF)
-            moves.append(pltpu.make_async_copy(out.at[slot], out_hbm.at[rows, cols], sems.at[slot]))
+    span = SIDE * COLS
+    bases = []
+    for at, (ref, dx) in enumerate(zip(parts, shifts)):
+        for dz in range(SIDE):
+            spot = pl.multiple_of(at * span + (col % SIDE - dz) % SIDE * COLS, COLS)
+            stacked[pl.ds(spot, COLS), :] = ref[dz]
+        bases.append(pl.ds(pl.multiple_of((col // SIDE - dx) % SIDE * span, span), span))
+    turned[...] = stacked[...].T
+    for n in range(s_ref.shape[1] // WIDE):
+        cols = pl.ds(n * WIDE, WIDE)
+        factor = jnp.concatenate([s_ref[base, cols] for base in bases], axis=0)
+        yield n, cols, mm(turned[...], factor)
+
+
+def half_scratch():
+    return [pltpu.VMEM((2 * SIDE * COLS, SR), BF), pltpu.VMEM((SR, 2 * SIDE * COLS), BF)]
+
+
+def final_first(near, far, factor, schur):
+    def body(w0, w1, s_ref, schur_ref, out_ref, stacked, turned):
+        for _, cols, change in change_blocks((w0, w1), (0, 1), s_ref, stacked, turned):
+            out_ref[:, cols] = schur_ref[:, cols].astype(F32) - change
+
+    return pl.pallas_call(
+        body,
+        in_specs=[vmem()] * 4,
+        out_specs=vmem(),
+        scratch_shapes=half_scratch(),
+        out_shape=jax.ShapeDtypeStruct(schur.shape, F32),
+        compiler_params=small(8),
+        name="final_first",
+    )(near, far, factor, schur)
+
+
+def final_second(parts, factor, partial):
+    def body(w2, w3, s_ref, part_ref, out_hbm, stacked, turned, out, sems):
+        moves = []
+        for n, cols, change in change_blocks((w2, w3), (2, 3), s_ref, stacked, turned):
+            slot = n % SIDE
+            if n >= SIDE:
+                moves[-SIDE].wait()
+            out[slot] = (part_ref[:, cols] - change).astype(BF)
+            moves.append(pltpu.make_async_copy(out.at[slot], out_hbm.at[:, cols], sems.at[slot]))
             moves[-1].start()
-    for move in moves[-4:]:
-        move.wait()
-
-
-def final(pieces, factor, schur):
-    return pl.pallas_call(
-        final_body,
-        in_specs=[vmem()] * 15,
+        for move in moves[-SIDE:]:
+            move.wait()
+
+    return pl.pallas_call(
+        body,
+        in_specs=[vmem()] * 4,
         out_specs=hbm(),
-        scratch_shapes=[
-            pltpu.VMEM((NRHS, SR), BF),
-            pltpu.VMEM((SR, NRHS), BF),
-            pltpu.VMEM((4, 256, 1024), BF),
-            pltpu.SemaphoreType.DMA((4,)),
-        ],
-        out_shape=jax.ShapeDtypeStruct(schur.shape, BF),
-        compiler_params=small(10),
-        name="final",
-    )(*pieces, factor, schur)
+        scratch_shapes=half_scratch() + [pltpu.VMEM((SIDE, SR, WIDE), BF), pltpu.SemaphoreType.DMA((SIDE,))],
+        out_shape=jax.ShapeDtypeStruct(partial.shape, BF),
+        compiler_params=small(12),
+        name="final_second",
+    )(*parts, factor, partial)
 
 
 def turned_cols(value, dx, dz):
@@ -310,32 +317,6 @@
 
 def gather_far(near):
     return [near] + [turned_cols(near, dx, 0) for dx in (1, 2, 3)]
-
-
-def stack_halves(pieces, first):
-    half = COLS // 2
-
-    def body(a, b, c, out_ref):
-        for at, ref in enumerate((a, b, c)):
-            out_ref[at] = ref[first : first + half, :]
-
-    return pl.pallas_call(
-        body,
-        in_specs=[vmem()] * 3,
-        out_specs=vmem(),
-        out_shape=jax.ShapeDtypeStruct((SIDE - 1, half, SR), BF),
-        compiler_params=small(2),
-    )(*pieces)
-
-
-def gather_cols(value):
-    half = COLS // 2
-    along_z = [turned_cols(value, 0, k) for k in (1, 2, 3)]
-    along_x = [turned_cols(value, k, 0) for k in (1, 2, 3)]
-    first = stack_halves(along_z, 0)
-    second = stack_halves(along_x, half)
-    others = [turned_cols(first, k, 0) for k in (1, 2, 3)] + [turned_cols(second, 0, k) for k in (1, 2, 3)]
-    return [value] + along_z + along_x + others
 
 
 def gather_chips(value, first):
@@ -377,7 +358,15 @@
     line = gather_chips(sent, dense)
     other = swap_cores(line)
     update = products_other(dense, other, products_own(dense, line))
-    return final(gather_cols(update), surface_factor, schur)
+    pieces = [update]
+    for k in (1, 2, 3):
+        pieces.append(turned_cols(update, 0, k))
+    near = jnp.stack(pieces)
+    far = []
+    for k in (1, 2, 3):
+        far.append(turned_cols(near, k, 0))
+    partial = final_first(near, far[0], surface_factor, schur)
+    return final_second([after(part, partial) for part in far[1:]], surface_factor, partial)
 
 
 def solution(mesh):

time: 83.6 us -> 78.5 us (0.939)
  starting transfers between devices: 43.2 us -> 37 us
  waiting for transfers between devices: 21.1 us -> 22.2 us
    ppermute x18 -> x12, starting transfers between devices: 25.4 us -> 19.2 us  [turned_cols(): return lax.ppermute(value, 'col', pairs)]
    ppermute x18 -> x12, waiting for transfers between devices: 16.5 us -> 17.5 us  [turned_cols(): return lax.ppermute(value, 'col', pairs)]
    pallas_call x3 -> x2, Pallas kernels: 5.77 us -> 5.83 us  [the longest x1 3.95 us: final_second(): pl.pallas_call(body, in_specs=[vmem()] * 4, out_specs=hbm(), scratch_shap...]
  transfers between devices with their start and end apart: 29 -> 23, of which waited for: 15 -> 10; matrix products, arithmetic and copies ran while one was open for 0% -> 0% of each run, Pallas kernels for 8% -> 10%
where the time goes in v1:
time: 78.5 us; the launch traced here: 78.3 us
  starting transfers between devices  37 us (47%)
  waiting for transfers between devices  22.2 us (28%)
  Pallas kernels  17.9 us (23%)
  between operations  1.14 us (1%)
    ppermute x12, starting transfers between devices, turned_cols(): return lax.ppermute(value, 'col', pairs)  19.2 us
    ppermute x12, waiting for transfers between devices, turned_cols(): return lax.ppermute(value, 'col', pairs)  17.5 us
    ppermute x3, starting transfers between devices, moved(): lax.ppermute(value, 'row', [(2 * a + c, 2 * ((a + k) % SIDE) + c) for a i...  12.2 us
    ppermute x7, starting transfers between devices, shards(): before = lax.ppermute(sent, 'row', [(step, step + 1)])  5.39 us
    pallas_call x1, Pallas kernels, final_second(): pl.pallas_call(body, in_specs=[vmem()] * 4, out_specs=hbm(), scratch_shap...  3.95 us
    pallas_call x1, Pallas kernels, prep(): pl.pallas_call(prep_body, in_specs=[hbm()] * 3, out_specs=[vmem()] * 5, o...  3.89 us
    ppermute x3, waiting for transfers between devices, moved(): lax.ppermute(value, 'row', [(2 * a + c, 2 * ((a + k) % SIDE) + c) for a i...  3.77 us
    pallas_call x1, Pallas kernels, build(): pl.pallas_call(build_body, in_specs=[vmem()] * 5, out_specs=vmem(), input...  2.33 us
  transfers between devices with their start and end apart: 23, of which 10 were waited for; matrix products, arithmetic and copies ran while one was open for 0% of the time, Pallas kernels for 10%

profile of v1, /device:TPU:0, one launch (start us, length us, event | category | flops | bytes accessed | tf_op | source)
XLA Modules:
  0.0 78.3 jit_solution(1061749910218856055)
XLA Ops:
  0.0 3.9 %prep.1 = (bf16[32,1024]{1,0:T(8,128)(2,1)S(1)}, bf16[1024,1024]{1,0:T(8,128)(2,1)S(1)}, bf16[1024,1024]{1,0:T(8,128)(2,1)S(1)}, bf16[1024,1024]{1,0:T(8,128)(2,1)S(1)}, bf16[1024,1024]{1,0:T(8,128)(2,1)S(1)}) custom-call(f32[32,1024]{1,0:T(8,128)} %rhs_ref.13, f32[1024,1024]{1,0:T(8,128)} %e_hbm.1, f32[1024,1024]{1,0:T(8,128)} %g_hbm.1), custom_call_target="tpu_custom_call" | custom-call | tf_op jit(solution)/shard_map/prep/pallas_call | solution.py:88
  3.9 1.3 %collective-permute-start = (bf16[32,1024]{1,0:T(8,128)(2,1)S(1)}, bf16[32,1024]{1,0:T(8,128)(2,1)S(1)}, u32[]{:S(2)}, u32[]{:S(2)}) collective-permute-start(bf16[32,1024]{1,0:T(8,128)(2,1)S(1)} %get-tuple-element.26.sent_ref), channel_id=1, source_target_pairs={{0,16},{1,17},{2,18},{3,19},{4,20},{5,21},{6,22},{7,23},{8,24},{9,... | collective-permute-start | bytes 196616 | tf_op jit(solution)/shard_map/ppermute | solution.py:341
  5.2 0.9 %collective-permute-done.before_ref = bf16[32,1024]{1,0:T(8,128)(2,1)S(1)} collective-permute-done((bf16[32,1024]{1,0:T(8,128)(2,1)S(1)}, bf16[32,1024]{1,0:T(8,128)(2,1)S(1)}, u32[]{:S(2)}, u32[]{:S(2)}) %collective-permute-start) | collective-permute-done | bytes 65568 | tf_op jit(solution)/shard_map/ppermute | solution.py:341
  6.1 0.8 %collective-permute-start.1 = (bf16[32,1024]{1,0:T(8,128)(2,1)S(1)}, bf16[32,1024]{1,0:T(8,128)(2,1)S(1)}, u32[]{:S(2)}, u32[]{:S(2)}) collective-permute-start(bf16[32,1024]{1,0:T(8,128)(2,1)S(1)} %shard_map.100.sent_ref), channel_id=1, source_target_pairs={{16,32},{17,33},{18,34},{19,35},{20,36},{21,37},{22,38},{23,39},{2... | collective-permute-start | bytes 196616 | tf_op jit(solution)/shard_map/ppermute | solution.py:341
  7.6 1.1 %pack.1 = bf16[13,16,128]{2,1,0:T(8,128)(2,1)S(1)} custom-call(s32[12]{0:T(128)S(1)} %copy-done.3, s32[12]{0:T(128)S(1)} %copy-done.4, s32[1]{0:T(128)S(6)} %copy.27.count, s32[1,48]{1,0:T(1,128)S(1)} %copy-done.5, bf16[12,16,128]{2,1,0:T(8,128)(2,1)S(1)} %copy-done.2), custom_call_target="tpu_custom_call" | custom-call | tf_op jit(solution)/shard_map/pack/pallas_call | solution.py:145
  8.8 0.7 collective-permute-start.2
  9.5 0.7 collective-permute-start.3
  10.2 4.7 %collective-permute-start.6 = (bf16[13,16,128]{2,1,0:T(8,128)(2,1)S(1)}, bf16[13,16,128]{2,1,0:T(8,128)(2,1)S(1)}, u32[]{:S(2)}, u32[]{:S(2)}) collective-permute-start(bf16[13,16,128]{2,1,0:T(8,128)(2,1)S(1)} %pack.1), channel_id=1, source_target_pairs={{0,3},{1,0},{2,1},{3,2},{4,7},{5,4},{6,5},{7,6},{8,11},{9,8},{10,9... | collective-permute-start | bytes 159752 | tf_op jit(solution)/shard_map/ppermute | solution.py:311
  14.9 1.3 %collective-permute-start.4 = (bf16[13,16,128]{2,1,0:T(8,128)(2,1)S(1)}, bf16[13,16,128]{2,1,0:T(8,128)(2,1)S(1)}, u32[]{:S(2)}, u32[]{:S(2)}) collective-permute-start(bf16[13,16,128]{2,1,0:T(8,128)(2,1)S(1)} %pack.1), channel_id=1, source_target_pairs={{0,1},{1,2},{2,3},{3,0},{4,5},{5,6},{6,7},{7,4},{8,9},{9,10},{10,1... | collective-permute-start | bytes 159752 | tf_op jit(solution)/shard_map/ppermute | solution.py:311
  16.6 3.9 %collective-permute-done.5 = bf16[13,16,128]{2,1,0:T(8,128)(2,1)S(1)} collective-permute-done((bf16[13,16,128]{2,1,0:T(8,128)(2,1)S(1)}, bf16[13,16,128]{2,1,0:T(8,128)(2,1)S(1)}, u32[]{:S(2)}, u32[]{:S(2)}) %collective-permute-start.5) | collective-permute-done | bytes 53280 | tf_op jit(solution)/shard_map/ppermute | solution.py:311
  20.8 2.8 %collective-permute-start.12 = (bf16[4,13,16,128]{3,2,1,0:T(8,128)(2,1)S(1)}, bf16[4,13,16,128]{3,2,1,0:T(8,128)(2,1)S(1)}, u32[]{:S(2)}, u32[]{:S(2)}) collective-permute-start(bf16[4,13,16,128]{3,2,1,0:T(8,128)(2,1)S(1)} %pad_maximum_fusion.1.c0), channel_id=1, source_target_pairs={{0,12},{1,13},{2,14},{3,15},{4,0},{5,1},{6,2},{7,3},{8,4},{9,5},{1... | collective-permute-start | bytes 638984 | tf_op jit(solution)/shard_map/ppermute | solution.py:311
  23.6 0.7 collective-permute-start.7
  24.3 0.9 %collective-permute-start.11 = (bf16[4,13,16,128]{3,2,1,0:T(8,128)(2,1)S(1)}, bf16[4,13,16,128]{3,2,1,0:T(8,128)(2,1)S(1)}, u32[]{:S(2)}, u32[]{:S(2)}) collective-permute-start(bf16[4,13,16,128]{3,2,1,0:T(8,128)(2,1)S(1)} %pad_maximum_fusion.1.c0), channel_id=1, source_target_pairs={{0,8},{1,9},{2,10},{3,11},{4,12},{5,13},{6,14},{7,15},{8,0},{9,1},... | collective-permute-start | bytes 638984 | tf_op jit(solution)/shard_map/ppermute | solution.py:311
  25.2 0.9 %collective-permute-start.8 = (bf16[4,13,16,128]{3,2,1,0:T(8,128)(2,1)S(1)}, bf16[4,13,16,128]{3,2,1,0:T(8,128)(2,1)S(1)}, u32[]{:S(2)}, u32[]{:S(2)}) collective-permute-start(bf16[4,13,16,128]{3,2,1,0:T(8,128)(2,1)S(1)} %pad_maximum_fusion.1.c0), channel_id=1, source_target_pairs={{0,4},{1,5},{2,6},{3,7},{4,8},{5,9},{6,10},{7,11},{8,12},{9,13},{1... | collective-permute-start | bytes 638984 | tf_op jit(solution)/shard_map/ppermute | solution.py:311
  26.1 0.7 collective-permute-start.9
  26.7 0.8 %clear.1.cleared = bf16[8,768,1024]{2,1,0:T(8,128)(2,1)S(1)} custom-call(bf16[32,1024]{1,0:T(8,128)(2,1)S(1)} %shard_map.104._.sent_ref), custom_call_target="tpu_custom_call" | custom-call | tf_op jit(solution)/shard_map/clear/pallas_call | solution.py:160
  27.6 0.7 collective-permute-start.10
  28.5 11.1 %collective-permute-start.15 = (bf16[32,1024]{1,0:T(8,128)(2,1)S(1)}, bf16[32,1024]{1,0:T(8,128)(2,1)S(1)}, u32[]{:S(2)}, u32[]{:S(2)}) collective-permute-start(bf16[32,1024]{1,0:T(8,128)(2,1)S(1)} %shard_map.106), channel_id=1, source_target_pairs={{0,96},{16,112},{32,0},{48,16},{64,32},{80,48},{96,64},{112,80},{1... | collective-permute-start | bytes 196616 | tf_op jit(solution)/shard_map/ppermute | solution.py:324
  39.6 1.1 %collective-permute-start.13 = (bf16[32,1024]{1,0:T(8,128)(2,1)S(1)}, bf16[32,1024]{1,0:T(8,128)(2,1)S(1)}, u32[]{:S(2)}, u32[]{:S(2)}) collective-permute-start(bf16[32,1024]{1,0:T(8,128)(2,1)S(1)} %shard_map.106), channel_id=1, source_target_pairs={{0,32},{16,48},{32,64},{48,80},{64,96},{80,112},{96,0},{112,16},{1... | collective-permute-start | bytes 196616 | tf_op jit(solution)/shard_map/ppermute | solution.py:324
  40.6 2.3 %build.1.c_ref = bf16[8,768,1024]{2,1,0:T(8,128)(2,1)S(1)} custom-call(bf16[8,768,1024]{2,1,0:T(8,128)(2,1)S(1)} %clear.1.cleared, bf16[4,13,16,128]{3,2,1,0:T(8,128)(2,1)S(1)} %pad_maximum_fusion.1.c0, bf16[4,13,16,128]{3,2,1,0:T(8,128)(2,1)S(1)} %collective-permute-done.8.c1, ...), custom_call_target="tpu_custom_call", output_to_operand_aliasing={{}: (0, {})} | custom-call | tf_op jit(solution)/shard_map/build/pallas_call | solution.py:191
  43.0 2.5 %collective-permute-done.14 = bf16[32,1024]{1,0:T(8,128)(2,1)S(1)} collective-permute-done((bf16[32,1024]{1,0:T(8,128)(2,1)S(1)}, bf16[32,1024]{1,0:T(8,128)(2,1)S(1)}, u32[]{:S(2)}, u32[]{:S(2)}) %collective-permute-start.14) | collective-permute-done | bytes 65568 | tf_op jit(solution)/shard_map/ppermute | solution.py:324
  45.5 1.3 %collective-permute-done.13 = bf16[32,1024]{1,0:T(8,128)(2,1)S(1)} collective-permute-done((bf16[32,1024]{1,0:T(8,128)(2,1)S(1)}, bf16[32,1024]{1,0:T(8,128)(2,1)S(1)}, u32[]{:S(2)}, u32[]{:S(2)}) %collective-permute-start.13) | collective-permute-done | bytes 65568 | tf_op jit(solution)/shard_map/ppermute | solution.py:324
  47.1 1.8 %products_own.1.sum_ref = f32[768,32]{1,0:T(8,128)S(1)} custom-call(bf16[8,768,1024]{2,1,0:T(8,128)(2,1)S(1)} %build.1.c_ref, bf16[4,32,1024]{2,1,0:T(8,128)(2,1)S(1)} %pad_maximum_fusion.x_ref), custom_call_target="tpu_custom_call" | custom-call | tf_op jit(solution)/shard_map/products_own/pallas_call | solution.py:228
  48.9 1.8 %products_other.1 = bf16[32,768]{1,0:T(8,128)(2,1)S(1)} custom-call(bf16[8,768,1024]{2,1,0:T(8,128)(2,1)S(1)} %build.1.c_ref, bf16[4,32,1024]{2,1,0:T(8,128)(2,1)S(1)} %collective-permute-done.16.x_ref, f32[768,32]{1,0:T(8,128)S(1)} %products_own.1.sum_ref), custom_call_target="tpu_custom_call" | custom-call | tf_op jit(solution)/shard_map/products_other/pallas_call | solution.py:239
  50.8 4.1 %collective-permute-start.19 = (bf16[32,768]{1,0:T(8,128)(2,1)S(1)}, bf16[32,768]{1,0:T(8,128)(2,1)S(1)}, u32[]{:S(2)}, u32[]{:S(2)}) collective-permute-start(bf16[32,768]{1,0:T(8,128)(2,1)S(1)} %products_other.1), channel_id=1, source_target_pairs={{0,3},{1,0},{2,1},{3,2},{4,7},{5,4},{6,5},{7,6},{8,11},{9,8},{10,9... | collective-permute-start | bytes 147464 | tf_op jit(solution)/shard_map/ppermute | solution.py:311
  54.8 1.3 %collective-permute-start.17 = (bf16[32,768]{1,0:T(8,128)(2,1)S(1)}, bf16[32,768]{1,0:T(8,128)(2,1)S(1)}, u32[]{:S(2)}, u32[]{:S(2)}) collective-permute-start(bf16[32,768]{1,0:T(8,128)(2,1)S(1)} %products_other.1), channel_id=1, source_target_pairs={{0,1},{1,2},{2,3},{3,0},{4,5},{5,6},{6,7},{7,4},{8,9},{9,10},{10,1... | collective-permute-start | bytes 147464 | tf_op jit(solution)/shard_map/ppermute | solution.py:311
  56.1 1.3 %collective-permute-done.19 = bf16[32,768]{1,0:T(8,128)(2,1)S(1)} collective-permute-done((bf16[32,768]{1,0:T(8,128)(2,1)S(1)}, bf16[32,768]{1,0:T(8,128)(2,1)S(1)}, u32[]{:S(2)}, u32[]{:S(2)}) %collective-permute-start.19) | collective-permute-done | bytes 49184 | tf_op jit(solution)/shard_map/ppermute | solution.py:311
  57.4 3.1 %collective-permute-done.18 = bf16[32,768]{1,0:T(8,128)(2,1)S(1)} collective-permute-done((bf16[32,768]{1,0:T(8,128)(2,1)S(1)}, bf16[32,768]{1,0:T(8,128)(2,1)S(1)}, u32[]{:S(2)}, u32[]{:S(2)}) %collective-permute-start.18) | collective-permute-done | bytes 49184 | tf_op jit(solution)/shard_map/ppermute | solution.py:311
  60.9 3.2 %collective-permute-start.22 = (bf16[4,32,768]{2,1,0:T(8,128)(2,1)S(1)}, bf16[4,32,768]{2,1,0:T(8,128)(2,1)S(1)}, u32[]{:S(2)}, u32[]{:S(2)}) collective-permute-start(bf16[4,32,768]{2,1,0:T(8,128)(2,1)S(1)} %pad_maximum_fusion.2.w0), channel_id=1, source_target_pairs={{0,12},{1,13},{2,14},{3,15},{4,0},{5,1},{6,2},{7,3},{8,4},{9,5},{1... | collective-permute-start | bytes 589832 | tf_op jit(solution)/shard_map/ppermute | solution.py:311
  64.1 8.2 %collective-permute-done.21.w1 = bf16[4,32,768]{2,1,0:T(8,128)(2,1)S(1)} collective-permute-done((bf16[4,32,768]{2,1,0:T(8,128)(2,1)S(1)}, bf16[4,32,768]{2,1,0:T(8,128)(2,1)S(1)}, u32[]{:S(2)}, u32[]{:S(2)}) %collective-permute-start.21) | collective-permute-done | bytes 196640 | tf_op jit(solution)/shard_map/ppermute | solution.py:311
  72.3 1.9 %final_first.1.part_ref = f32[768,4096]{1,0:T(8,128)S(1)} custom-call(bf16[4,32,768]{2,1,0:T(8,128)(2,1)S(1)} %pad_maximum_fusion.2.w0, bf16[4,32,768]{2,1,0:T(8,128)(2,1)S(1)} %collective-permute-done.21.w1, bf16[512,4096]{1,0:T(8,128)(2,1)S(1)} %copy-done, bf16[768,4096]{1,0:T(8,128)(2,1)S(1)} %bitcast.13), custom_call_target="tpu_custom_call" | custom-call | tf_op jit(solution)/shard_map/final_first/pallas_call | solution.py:274
  74.2 3.9 %final_second.1 = bf16[768,4096]{1,0:T(8,128)(2,1)} custom-call(bf16[4,32,768]{2,1,0:T(8,128)(2,1)S(1)} %collective-permute-done.20.w2, bf16[4,32,768]{2,1,0:T(8,128)(2,1)S(1)} %collective-permute-done.22.w3, bf16[512,4096]{1,0:T(8,128)(2,1)S(1)} %copy-done, f32[768,4096]{1,0:T(8,128)S(1)} %final_first.1.part_ref), custom_call_target="tpu_custom_call" | custom-call | tf_op jit(solution)/shard_map/final_second/pallas_call | solution.py:298
  (49 shorter events, 1.8 us)
Async XLA Ops:
  0.0 6.1 %copy-start.1 = (f32[32,1024]{1,0:T(8,128)S(1)}, f32[32,1024]{1,0:T(8,128)}, u32[]{:S(2)}) copy-start(f32[32,1024]{1,0:T(8,128)} %rhs_ref.13) | copy-start | bytes 393220
  3.9 2.2 %collective-permute-start = (bf16[32,1024]{1,0:T(8,128)(2,1)S(1)}, bf16[32,1024]{1,0:T(8,128)(2,1)S(1)}, u32[]{:S(2)}, u32[]{:S(2)}) collective-permute-start(bf16[32,1024]{1,0:T(8,128)(2,1)S(1)} %get-tuple-element.26.sent_ref), channel_id=1, source_target_pairs={{0,16},{1,17},{2,18},{3,19},{4,20},{5,21},{6,22},{7,23},{8,24},{9,... | collective-permute-start | bytes 196616 | tf_op jit(solution)/shard_map/ppermute | solution.py:341
  6.1 1.5 %copy-start.2 = (bf16[12,16,128]{2,1,0:T(8,128)(2,1)S(1)}, bf16[12,16,128]{2,1,0:T(8,128)(2,1)}, u32[]{:S(2)}) copy-start(bf16[12,16,128]{2,1,0:T(8,128)(2,1)} %coupling_ref) | copy-start | bytes 147460
  6.1 1.5 %copy-start.3 = (s32[12]{0:T(128)S(1)}, s32[12]{0:T(128)}, u32[]{:S(2)}) copy-start(s32[12]{0:T(128)} %blocks.1) | copy-start | bytes 148
  6.1 1.5 %copy-start.4 = (s32[12]{0:T(128)S(1)}, s32[12]{0:T(128)}, u32[]{:S(2)}) copy-start(s32[12]{0:T(128)} %tiles.1) | copy-start | bytes 148
  6.1 1.5 %copy-start.5 = (s32[1,48]{1,0:T(1,128)S(1)}, s32[1,48]{1,0:T(1,128)}, u32[]{:S(2)}) copy-start(s32[1,48]{1,0:T(1,128)} %slots.1) | copy-start | bytes 580
  6.1 2.6 %collective-permute-start.1 = (bf16[32,1024]{1,0:T(8,128)(2,1)S(1)}, bf16[32,1024]{1,0:T(8,128)(2,1)S(1)}, u32[]{:S(2)}, u32[]{:S(2)}) collective-permute-start(bf16[32,1024]{1,0:T(8,128)(2,1)S(1)} %shard_map.100.sent_ref), channel_id=1, source_target_pairs={{16,32},{17,33},{18,34},{19,35},{20,36},{21,37},{22,38},{23,39},{2... | collective-permute-start | bytes 196616 | tf_op jit(solution)/shard_map/ppermute | solution.py:341
  8.8 0.7 collective-permute-start.2
  9.5 11.3 %collective-permute-start.3 = (bf16[32,1024]{1,0:T(8,128)(2,1)S(1)}, bf16[32,1024]{1,0:T(8,128)(2,1)S(1)}, u32[]{:S(2)}, u32[]{:S(2)}) collective-permute-start(bf16[32,1024]{1,0:T(8,128)(2,1)S(1)} %shard_map.102.sent_ref), channel_id=1, source_target_pairs={{48,64},{49,65},{50,66},{51,67},{52,68},{53,69},{54,70},{55,71},{5... | collective-permute-start | bytes 196616 | tf_op jit(solution)/shard_map/ppermute | solution.py:341
  10.2 6.5 %collective-permute-start.6 = (bf16[13,16,128]{2,1,0:T(8,128)(2,1)S(1)}, bf16[13,16,128]{2,1,0:T(8,128)(2,1)S(1)}, u32[]{:S(2)}, u32[]{:S(2)}) collective-permute-start(bf16[13,16,128]{2,1,0:T(8,128)(2,1)S(1)} %pack.1), channel_id=1, source_target_pairs={{0,3},{1,0},{2,1},{3,2},{4,7},{5,4},{6,5},{7,6},{8,11},{9,8},{10,9... | collective-permute-start | bytes 159752 | tf_op jit(solution)/shard_map/ppermute | solution.py:311
  14.8 5.7 %collective-permute-start.5 = (bf16[13,16,128]{2,1,0:T(8,128)(2,1)S(1)}, bf16[13,16,128]{2,1,0:T(8,128)(2,1)S(1)}, u32[]{:S(2)}, u32[]{:S(2)}) collective-permute-start(bf16[13,16,128]{2,1,0:T(8,128)(2,1)S(1)} %pack.1), channel_id=1, source_target_pairs={{0,2},{1,3},{2,0},{3,1},{4,6},{5,7},{6,4},{7,5},{8,10},{9,11},{10,... | collective-permute-start | bytes 159752 | tf_op jit(solution)/shard_map/ppermute | solution.py:311
  14.9 5.9 %collective-permute-start.4 = (bf16[13,16,128]{2,1,0:T(8,128)(2,1)S(1)}, bf16[13,16,128]{2,1,0:T(8,128)(2,1)S(1)}, u32[]{:S(2)}, u32[]{:S(2)}) collective-permute-start(bf16[13,16,128]{2,1,0:T(8,128)(2,1)S(1)} %pack.1), channel_id=1, source_target_pairs={{0,1},{1,2},{2,3},{3,0},{4,5},{5,6},{6,7},{7,4},{8,9},{9,10},{10,1... | collective-permute-start | bytes 159752 | tf_op jit(solution)/shard_map/ppermute | solution.py:311
  20.8 18.8 %collective-permute-start.12 = (bf16[4,13,16,128]{3,2,1,0:T(8,128)(2,1)S(1)}, bf16[4,13,16,128]{3,2,1,0:T(8,128)(2,1)S(1)}, u32[]{:S(2)}, u32[]{:S(2)}) collective-permute-start(bf16[4,13,16,128]{3,2,1,0:T(8,128)(2,1)S(1)} %pad_maximum_fusion.1.c0), channel_id=1, source_target_pairs={{0,12},{1,13},{2,14},{3,15},{4,0},{5,1},{6,2},{7,3},{8,4},{9,5},{1... | collective-permute-start | bytes 638984 | tf_op jit(solution)/shard_map/ppermute | solution.py:311
  23.6 2.4 %collective-permute-start.7 = (bf16[32,1024]{1,0:T(8,128)(2,1)S(1)}, bf16[32,1024]{1,0:T(8,128)(2,1)S(1)}, u32[]{:S(2)}, u32[]{:S(2)}) collective-permute-start(bf16[32,1024]{1,0:T(8,128)(2,1)S(1)} %shard_map.103.sent_ref), channel_id=1, source_target_pairs={{64,80},{65,81},{66,82},{67,83},{68,84},{69,85},{70,86},{71,87},{7... | collective-permute-start | bytes 196616 | tf_op jit(solution)/shard_map/ppermute | solution.py:341
  24.3 16.3 %collective-permute-start.11 = (bf16[4,13,16,128]{3,2,1,0:T(8,128)(2,1)S(1)}, bf16[4,13,16,128]{3,2,1,0:T(8,128)(2,1)S(1)}, u32[]{:S(2)}, u32[]{:S(2)}) collective-permute-start(bf16[4,13,16,128]{3,2,1,0:T(8,128)(2,1)S(1)} %pad_maximum_fusion.1.c0), channel_id=1, source_target_pairs={{0,8},{1,9},{2,10},{3,11},{4,12},{5,13},{6,14},{7,15},{8,0},{9,1},... | collective-permute-start | bytes 638984 | tf_op jit(solution)/shard_map/ppermute | solution.py:311
  25.2 15.5 %collective-permute-start.8 = (bf16[4,13,16,128]{3,2,1,0:T(8,128)(2,1)S(1)}, bf16[4,13,16,128]{3,2,1,0:T(8,128)(2,1)S(1)}, u32[]{:S(2)}, u32[]{:S(2)}) collective-permute-start(bf16[4,13,16,128]{3,2,1,0:T(8,128)(2,1)S(1)} %pad_maximum_fusion.1.c0), channel_id=1, source_target_pairs={{0,4},{1,5},{2,6},{3,7},{4,8},{5,9},{6,10},{7,11},{8,12},{9,13},{1... | collective-permute-start | bytes 638984 | tf_op jit(solution)/shard_map/ppermute | solution.py:311
  26.1 1.5 %collective-permute-start.9 = (bf16[32,1024]{1,0:T(8,128)(2,1)S(1)}, bf16[32,1024]{1,0:T(8,128)(2,1)S(1)}, u32[]{:S(2)}, u32[]{:S(2)}) collective-permute-start(bf16[32,1024]{1,0:T(8,128)(2,1)S(1)} %shard_map.104._.sent_ref), channel_id=1, source_target_pairs={{80,96},{81,97},{82,98},{83,99},{84,100},{85,101},{86,102},{87,103... | collective-permute-start | bytes 196616 | tf_op jit(solution)/shard_map/ppermute | solution.py:341
  27.6 0.7 collective-permute-start.10
  28.5 14.5 %collective-permute-start.15 = (bf16[32,1024]{1,0:T(8,128)(2,1)S(1)}, bf16[32,1024]{1,0:T(8,128)(2,1)S(1)}, u32[]{:S(2)}, u32[]{:S(2)}) collective-permute-start(bf16[32,1024]{1,0:T(8,128)(2,1)S(1)} %shard_map.106), channel_id=1, source_target_pairs={{0,96},{16,112},{32,0},{48,16},{64,32},{80,48},{96,64},{112,80},{1... | collective-permute-start | bytes 196616 | tf_op jit(solution)/shard_map/ppermute | solution.py:324
  39.6 5.9 %collective-permute-start.14 = (bf16[32,1024]{1,0:T(8,128)(2,1)S(1)}, bf16[32,1024]{1,0:T(8,128)(2,1)S(1)}, u32[]{:S(2)}, u32[]{:S(2)}) collective-permute-start(bf16[32,1024]{1,0:T(8,128)(2,1)S(1)} %shard_map.106), channel_id=1, source_target_pairs={{0,64},{16,80},{32,96},{48,112},{64,0},{80,16},{96,32},{112,48},{1... | collective-permute-start | bytes 196616 | tf_op jit(solution)/shard_map/ppermute | solution.py:324
  39.6 7.2 %collective-permute-start.13 = (bf16[32,1024]{1,0:T(8,128)(2,1)S(1)}, bf16[32,1024]{1,0:T(8,128)(2,1)S(1)}, u32[]{:S(2)}, u32[]{:S(2)}) collective-permute-start(bf16[32,1024]{1,0:T(8,128)(2,1)S(1)} %shard_map.106), channel_id=1, source_target_pairs={{0,32},{16,48},{32,64},{48,80},{64,96},{80,112},{96,0},{112,16},{1... | collective-permute-start | bytes 196616 | tf_op jit(solution)/shard_map/ppermute | solution.py:324
  46.8 2.1 %collective-permute-start.16 = (bf16[4,32,1024]{2,1,0:T(8,128)(2,1)S(1)}, bf16[4,32,1024]{2,1,0:T(8,128)(2,1)S(1)}, u32[]{:S(2)}, u32[]{:S(2)}) collective-permute-start(bf16[4,32,1024]{2,1,0:T(8,128)(2,1)S(1)} %pad_maximum_fusion.x_ref), channel_id=1, source_target_pairs={{0,16},{16,0},{32,48},{48,32},{64,80},{80,64},{96,112},{112,96},{1... | collective-permute-start | bytes 786440 | tf_op jit(solution)/shard_map/ppermute | solution.py:330
  47.1 25.2 %slice-start = ((s8[6291456]{0:T(1024)(128)(4,1)}), s8[4194304]{0:T(1024)(128)(4,1)S(1)}, s32[]{:S(2)}) async-start(s8[6291456]{0:T(1024)(128)(4,1)} %bitcast.12), calls=%async_computation | async-start | bytes 8388608
  48.9 23.4 %copy-start = (bf16[512,4096]{1,0:T(8,128)(2,1)S(1)}, bf16[512,4096]{1,0:T(8,128)(2,1)}, u32[]{:S(2)}) copy-start(bf16[512,4096]{1,0:T(8,128)(2,1)} %s_ref.3) | copy-start | bytes 12582916
  48.9 23.4 %slice-start.1 = ((s8[6291456]{0:T(1024)(128)(4,1)}), s8[2097152]{0:T(1024)(128)(4,1)S(1)}, s32[]{:S(2)}) async-start(s8[6291456]{0:T(1024)(128)(4,1)} %bitcast.12), calls=%async_computation.1 | async-start | bytes 4194304
  50.8 6.6 %collective-permute-start.19 = (bf16[32,768]{1,0:T(8,128)(2,1)S(1)}, bf16[32,768]{1,0:T(8,128)(2,1)S(1)}, u32[]{:S(2)}, u32[]{:S(2)}) collective-permute-start(bf16[32,768]{1,0:T(8,128)(2,1)S(1)} %products_other.1), channel_id=1, source_target_pairs={{0,3},{1,0},{2,1},{3,2},{4,7},{5,4},{6,5},{7,6},{8,11},{9,8},{10,9... | collective-permute-start | bytes 147464 | tf_op jit(solution)/shard_map/ppermute | solution.py:311
  54.8 5.7 %collective-permute-start.18 = (bf16[32,768]{1,0:T(8,128)(2,1)S(1)}, bf16[32,768]{1,0:T(8,128)(2,1)S(1)}, u32[]{:S(2)}, u32[]{:S(2)}) collective-permute-start(bf16[32,768]{1,0:T(8,128)(2,1)S(1)} %products_other.1), channel_id=1, source_target_pairs={{0,2},{1,3},{2,0},{3,1},{4,6},{5,7},{6,4},{7,5},{8,10},{9,11},{10,... | collective-permute-start | bytes 147464 | tf_op jit(solution)/shard_map/ppermute | solution.py:311
  54.8 5.9 %collective-permute-start.17 = (bf16[32,768]{1,0:T(8,128)(2,1)S(1)}, bf16[32,768]{1,0:T(8,128)(2,1)S(1)}, u32[]{:S(2)}, u32[]{:S(2)}) collective-permute-start(bf16[32,768]{1,0:T(8,128)(2,1)S(1)} %products_other.1), channel_id=1, source_target_pairs={{0,1},{1,2},{2,3},{3,0},{4,5},{5,6},{6,7},{7,4},{8,9},{9,10},{10,1... | collective-permute-start | bytes 147464 | tf_op jit(solution)/shard_map/ppermute | solution.py:311
  60.8 11.5 %collective-permute-start.21 = (bf16[4,32,768]{2,1,0:T(8,128)(2,1)S(1)}, bf16[4,32,768]{2,1,0:T(8,128)(2,1)S(1)}, u32[]{:S(2)}, u32[]{:S(2)}) collective-permute-start(bf16[4,32,768]{2,1,0:T(8,128)(2,1)S(1)} %pad_maximum_fusion.2.w0), channel_id=1, source_target_pairs={{0,4},{1,5},{2,6},{3,7},{4,8},{5,9},{6,10},{7,11},{8,12},{9,13},{1... | collective-permute-start | bytes 589832 | tf_op jit(solution)/shard_map/ppermute | solution.py:311
  60.9 13.3 %collective-permute-start.22 = (bf16[4,32,768]{2,1,0:T(8,128)(2,1)S(1)}, bf16[4,32,768]{2,1,0:T(8,128)(2,1)S(1)}, u32[]{:S(2)}, u32[]{:S(2)}) collective-permute-start(bf16[4,32,768]{2,1,0:T(8,128)(2,1)S(1)} %pad_maximum_fusion.2.w0), channel_id=1, source_target_pairs={{0,12},{1,13},{2,14},{3,15},{4,0},{5,1},{6,2},{7,3},{8,4},{9,5},{1... | collective-permute-start | bytes 589832 | tf_op jit(solution)/shard_map/ppermute | solution.py:311
  64.1 10.1 %collective-permute-start.20 = (bf16[4,32,768]{2,1,0:T(8,128)(2,1)S(1)}, bf16[4,32,768]{2,1,0:T(8,128)(2,1)S(1)}, u32[]{:S(2)}, u32[]{:S(2)}) collective-permute-start(bf16[4,32,768]{2,1,0:T(8,128)(2,1)S(1)} %pad_maximum_fusion.2.w0), channel_id=1, source_target_pairs={{0,8},{1,9},{2,10},{3,11},{4,12},{5,13},{6,14},{7,15},{8,0},{9,1},... | collective-permute-start | bytes 589832 | tf_op jit(solution)/shard_map/ppermute | solution.py:311

commit v2 on v1

--- a/solution.py
+++ b/solution.py
@@ -63,60 +63,131 @@
     return both[: left.shape[0]] + both[left.shape[0] :] + mm(first, low)
 
 
-def prep_body(rhs_hbm, e_hbm, g_hbm, sent_ref, e_high, e_low, g_high, g_low, rhs_in, e_in, g_in, sems):
+def loads(source, target, sems, first, skip):
     rows = NB // CHUNKS
-    moves = [pltpu.make_async_copy(rhs_hbm, rhs_in, sems.at[0])]
-    for source, target in ((g_hbm, g_in), (e_hbm, e_in)):
-        for at in range(CHUNKS):
-            piece = pl.ds(at * rows, rows)
-            moves.append(pltpu.make_async_copy(source.at[piece], target.at[piece], sems.at[len(moves)]))
-    for move in moves:
-        move.start()
-    for at in range(CHUNKS):
+    moves = []
+    for at in range(target.shape[0] // rows):
+        piece = source.at[pl.ds(skip + at * rows, rows)]
+        moves.append(pltpu.make_async_copy(piece, target.at[pl.ds(at * rows, rows)], sems.at[first + at]))
+        moves[-1].start()
+    return moves
+
+
+def split_arriving(moves, source, high_ref, low_ref):
+    rows = NB // CHUNKS
+    for at, move in enumerate(moves):
         piece = pl.ds(at * rows, rows)
-        moves[1 + at].wait()
-        g_high[piece], g_low[piece] = split(g_in[piece])
-    moves[0].wait()
+        move.wait()
+        high_ref[piece], low_ref[piece] = split(source[piece])
+
+
+def first_body(rhs_hbm, e_hbm, g_hbm, sent_ref, g_high, g_low, e_high, e_low, rhs_in, e_in, g_in, sems):
+    fetch = pltpu.make_async_copy(rhs_hbm, rhs_in, sems.at[0])
+    fetch.start()
+    g_moves = loads(g_hbm, g_in, sems, 1, 0)
+    e_moves = loads(e_hbm, e_in, sems, 1 + CHUNKS, 0)
+    split_arriving(g_moves, g_in, g_high, g_low)
+    fetch.wait()
     sent_ref[...] = with_split(rhs_in[...], g_high[...], g_low[...]).astype(BF)
-    for at in range(CHUNKS):
-        piece = pl.ds(at * rows, rows)
-        moves[1 + CHUNKS + at].wait()
-        e_high[piece], e_low[piece] = split(e_in[piece])
-
-
-def prep(rhs, lower, inverse):
-    return pl.pallas_call(
-        prep_body,
+    split_arriving(e_moves, e_in, e_high, e_low)
+
+
+def second_body(e_hbm, _, e_high, e_low, e_in, sems):
+    split_arriving(loads(e_hbm, e_in, sems, 0, NB // 2), e_in, e_high, e_low)
+
+
+def prep_first(rhs, lower, inverse):
+    half = NB // 2
+    return pl.pallas_call(
+        first_body,
         in_specs=[hbm()] * 3,
         out_specs=[vmem()] * 5,
-        out_shape=[shape(COLS)] + [shape(NB)] * 4,
+        out_shape=[shape(COLS), shape(NB), shape(NB), shape(half), shape(half)],
         scratch_shapes=[
             pltpu.VMEM((COLS, NB), F32),
-            pltpu.VMEM((NB, NB), F32),
+            pltpu.VMEM((half, NB), F32),
             pltpu.VMEM((NB, NB), F32),
             pltpu.SemaphoreType.DMA((1 + 2 * CHUNKS,)),
         ],
         compiler_params=small(12),
-        name="prep",
+        name="prep_first",
     )(in_hbm(rhs), in_hbm(lower), in_hbm(inverse))
 
 
+def prep_second(lower, earlier):
+    half = NB // 2
+    return pl.pallas_call(
+        second_body,
+        in_specs=[hbm(), pl.BlockSpec(memory_space=pl.ANY)],
+        out_specs=[vmem()] * 2,
+        out_shape=[shape(half)] * 2,
+        scratch_shapes=[pltpu.VMEM((half, NB), F32), pltpu.SemaphoreType.DMA((CHUNKS,))],
+        compiler_params=small(8),
+        name="prep_second",
+    )(in_hbm(lower), earlier)
+
+
+def change_body(rhs_ref, g_high, g_low, e0, e1, e2, e3, y_ref, high_ref, low_ref):
+    rows, half = NB // CHUNKS, NB // 2
+
+    @pl.when(lax.axis_index("row") == N_ROW - 1)
+    def _():
+        y_ref[...] = with_split(rhs_ref[...], g_high[...], g_low[...])
+        for at in range(CHUNKS):
+            high_e, low_e = (e0, e1) if at * rows < half else (e2, e3)
+            piece = pl.ds(at * rows % half, rows)
+            high, low = high_e[piece], low_e[piece]
+            change = mm(high, g_high[...]) + mm(high, g_low[...]) + mm(low, g_high[...])
+            high_ref[pl.ds(at * rows, rows)], low_ref[pl.ds(at * rows, rows)] = split(-change)
+
+
+def change_of(rhs, factors):
+    return pl.pallas_call(
+        change_body,
+        in_specs=[vmem()] * 7,
+        out_specs=[vmem()] * 3,
+        out_shape=[shape(COLS, F32), shape(NB), shape(NB)],
+        compiler_params=small(10),
+        name="change",
+    )(rhs, *factors)
+
+
 def advance(step, sent, before, rhs, factors):
-    def body(sent_ref, rhs_ref, before_ref, e_high, e_low, g_high, g_low, out_ref):
+    def body(sent_ref, rhs_ref, before_ref, g_high, g_low, e0, e1, e2, e3, out_ref):
+        half = NB // 2
+
         @pl.when(lax.axis_index("row") == step + 1)
         def _():
-            moved = before_ref[...]
-            right = rhs_ref[...] - mm(moved, e_high[...]) - mm(moved, e_low[...])
+            upper, lower = before_ref[:, :half], before_ref[:, half:]
+            right = rhs_ref[...] - mm(upper, e0[...]) - mm(upper, e1[...]) - mm(lower, e2[...]) - mm(lower, e3[...])
             out_ref[...] = with_split(right, g_high[...], g_low[...]).astype(BF)
 
     return pl.pallas_call(
         body,
-        in_specs=[vmem()] * 7,
+        in_specs=[vmem()] * 9,
         out_specs=vmem(),
         out_shape=shape(COLS),
         input_output_aliases={0: 0},
         compiler_params=small(4),
     )(sent, rhs, before, *factors)
+
+
+def advance_last(sent, before, y, high, low):
+    def body(sent_ref, y_ref, before_ref, high_ref, low_ref, out_ref):
+        @pl.when(lax.axis_index("row") == N_ROW - 1)
+        def _():
+            moved = before_ref[...]
+            out_ref[...] = (y_ref[...] + mm(moved, high_ref[...]) + mm(moved, low_ref[...])).astype(BF)
+
+    return pl.pallas_call(
+        body,
+        in_specs=[vmem()] * 5,
+        out_specs=vmem(),
+        out_shape=shape(COLS),
+        input_output_aliases={0: 0},
+        compiler_params=small(4),
+        name="advance_last",
+    )(sent, y, before, high, low)
 
 
 def pack_body(blocks, tiles, count, slots, coupling_ref, out_ref, place):
@@ -204,35 +275,31 @@
     )(cleared, *parts)
 
 
-def line_sum(other, c_ref, x_ref):
-    row = lax.axis_index("row")
-    chip, core = row // 2, row % 2
-    side = 1 - core if other else core
-    total = None
-    for k in range(SIDE):
-        group = 2 * ((chip - k) % SIDE) + side
-        part = lax.dot_general(c_ref[group], x_ref[k], (((1,), (1,)), ((), ())), preferred_element_type=F32)
-        total = part if total is None else total + part
-    return total
-
-
-def own_body(c_ref, x_ref, out_ref):
-    out_ref[...] = line_sum(False, c_ref, x_ref)
-
-
-def other_body(c_ref, x_ref, sum_ref, out_ref):
-    out_ref[...] = (sum_ref[...] + line_sum(True, c_ref, x_ref)).T.astype(BF)
-
-
-def products_own(dense, line):
-    return pl.pallas_call(
-        own_body,
-        in_specs=[vmem()] * 2,
+def group_product(c_ref, x, k, side):
+    group = 2 * ((lax.axis_index("row") // 2 - k) % SIDE) + side
+    return lax.dot_general(c_ref[group], x, (((1,), (1,)), ((), ())), preferred_element_type=F32)
+
+
+def product_own(dense, x, k, sums=None):
+    def body(c_ref, x_ref, *refs):
+        part = group_product(c_ref, x_ref[...], k, lax.axis_index("row") % 2)
+        refs[-1][...] = part if len(refs) == 1 else refs[0][...] + part
+
+    more = () if sums is None else (sums,)
+    return pl.pallas_call(
+        body,
+        in_specs=[vmem()] * (2 + len(more)),
         out_specs=vmem(),
         out_shape=jax.ShapeDtypeStruct((SR, COLS), F32),
         compiler_params=small(4),
-        name="products_own",
-    )(dense, line)
+    )(dense, x, *more)
+
+
+def other_body(c_ref, x_ref, sum_ref, out_ref):
+    total = sum_ref[...]
+    for k in range(SIDE):
+        total = total + group_product(c_ref, x_ref[k], k, 1 - lax.axis_index("row") % 2)
+    out_ref[...] = total.T.astype(BF)
 
 
 def products_other(dense, line, sums):
@@ -255,11 +322,17 @@
             spot = pl.multiple_of(at * span + (col % SIDE - dz) % SIDE * COLS, COLS)
             stacked[pl.ds(spot, COLS), :] = ref[dz]
         bases.append(pl.ds(pl.multiple_of((col // SIDE - dx) % SIDE * span, span), span))
-    turned[...] = stacked[...].T
+    tall = SR // 3
     for n in range(s_ref.shape[1] // WIDE):
         cols = pl.ds(n * WIDE, WIDE)
         factor = jnp.concatenate([s_ref[base, cols] for base in bases], axis=0)
-        yield n, cols, mm(turned[...], factor)
+        if n == 0:
+            for m in range(3):
+                rows = pl.ds(m * tall, tall)
+                turned[rows, :] = stacked[:, rows].T
+                yield n, m, rows, cols, mm(turned[rows, :], factor)
+        else:
+            yield n, 0, pl.ds(0, SR), cols, mm(turned[...], factor)
 
 
 def half_scratch():
@@ -268,8 +341,8 @@
 
 def final_first(near, far, factor, schur):
     def body(w0, w1, s_ref, schur_ref, out_ref, stacked, turned):
-        for _, cols, change in change_blocks((w0, w1), (0, 1), s_ref, stacked, turned):
-            out_ref[:, cols] = schur_ref[:, cols].astype(F32) - change
+        for _, _, rows, cols, change in change_blocks((w0, w1), (0, 1), s_ref, stacked, turned):
+            out_ref[rows, cols] = schur_ref[rows, cols].astype(F32) - change
 
     return pl.pallas_call(
         body,
@@ -284,22 +357,24 @@
 
 def final_second(parts, factor, partial):
     def body(w2, w3, s_ref, part_ref, out_hbm, stacked, turned, out, sems):
-        moves = []
-        for n, cols, change in change_blocks((w2, w3), (2, 3), s_ref, stacked, turned):
+        moves = {}
+        for n, m, rows, cols, change in change_blocks((w2, w3), (2, 3), s_ref, stacked, turned):
             slot = n % SIDE
-            if n >= SIDE:
-                moves[-SIDE].wait()
-            out[slot] = (part_ref[:, cols] - change).astype(BF)
-            moves.append(pltpu.make_async_copy(out.at[slot], out_hbm.at[:, cols], sems.at[slot]))
-            moves[-1].start()
-        for move in moves[-SIDE:]:
-            move.wait()
+            for move in moves.pop(n - SIDE, ()):
+                move.wait()
+            out[slot, rows] = (part_ref[rows, cols] - change).astype(BF)
+            move = pltpu.make_async_copy(out.at[slot, rows], out_hbm.at[rows, cols], sems.at[slot, m])
+            move.start()
+            moves.setdefault(n, []).append(move)
+        for group in moves.values():
+            for move in group:
+                move.wait()
 
     return pl.pallas_call(
         body,
         in_specs=[vmem()] * 4,
         out_specs=hbm(),
-        scratch_shapes=half_scratch() + [pltpu.VMEM((SIDE, SR, WIDE), BF), pltpu.SemaphoreType.DMA((SIDE,))],
+        scratch_shapes=half_scratch() + [pltpu.VMEM((SIDE, SR, WIDE), BF), pltpu.SemaphoreType.DMA((SIDE, 3))],
         out_shape=jax.ShapeDtypeStruct(partial.shape, BF),
         compiler_params=small(12),
         name="final_second",
@@ -319,11 +394,8 @@
     return [near] + [turned_cols(near, dx, 0) for dx in (1, 2, 3)]
 
 
-def gather_chips(value, first):
-    def moved(k):
-        return lax.ppermute(value, "row", [(2 * a + c, 2 * ((a + k) % SIDE) + c) for a in range(SIDE) for c in (0, 1)])
-
-    return jnp.stack([value] + [after(moved(k), first) for k in (1, 2, 3)])
+def chip_shift(value, k):
+    return lax.ppermute(value, "row", [(2 * a + c, 2 * ((a + k) % SIDE) + c) for a in range(SIDE) for c in (0, 1)])
 
 
 def swap_cores(value):
@@ -335,10 +407,13 @@
 
 
 def shards(rhs, couple_prev, diag_inverse, coupling, pair_block, pair_tile, pair_count, owner_slot, schur, surface_factor):
-    sent, *factors = prep(rhs, couple_prev, diag_inverse)
-    near = parts = packed = cleared = None
+    sent, g_high, g_low, *upper = prep_first(rhs, couple_prev, diag_inverse)
+    factors = (g_high, g_low, *upper, *prep_second(couple_prev, sent))
+    near = parts = packed = cleared = last = None
     for step in range(N_ROW - 1):
         before = lax.ppermute(sent, "row", [(step, step + 1)])
+        if step == 0:
+            before = after(before, factors[-1])
         if step == 1:
             packed = pack(after(coupling, sent), pair_block, pair_tile, pair_count, owner_slot)
             before = after(before, packed)
@@ -351,13 +426,22 @@
             parts = gather_far(near)
             before = after(before, near)
         if step == 5:
+            last = change_of(after(rhs, sent), factors)
+            before = after(before, last)
+        if step == 6:
             cleared = clear(sent)
             before = after(before, cleared)
-        sent = advance(step, sent, before, rhs, factors)
+        if step < N_ROW - 2:
+            sent = advance(step, sent, before, rhs, factors)
+        else:
+            sent = advance_last(sent, before, *last)
     dense = build([parts[0]] + [after(part, sent) for part in parts[1:]], cleared)
-    line = gather_chips(sent, dense)
-    other = swap_cores(line)
-    update = products_other(dense, other, products_own(dense, line))
+    line = [sent] + [chip_shift(sent, k) for k in (1, 2, 3)]
+    sums = product_own(dense, sent, 0)
+    for k in (1, 3, 2):
+        line[k] = after(line[k], sums)
+        sums = product_own(dense, line[k], k, sums)
+    update = products_other(dense, swap_cores(jnp.stack(line)), sums)
     pieces = [update]
     for k in (1, 2, 3):
         pieces.append(turned_cols(update, 0, k))

time: 78.5 us -> 77.3 us (0.985)
  waiting for transfers between devices: 22.2 us -> 19.5 us
  Pallas kernels: 17.9 us -> 19.8 us
    ppermute x3, waiting for transfers between devices: 3.77 us -> 0.91 us  [chip_shift(): lax.ppermute(value, 'row', [(2 * a + c, 2 * ((a + k) % SIDE) + c) for a i...]
    pallas_call x9 -> x14, Pallas kernels: 5.93 us -> 7.84 us  [the longest x1 3.58 us: prep_first(): pl.pallas_call(first_body, in_specs=[hbm()] * 3, out_specs=[vmem()] * 5,...]
    ppermute x1, waiting for transfers between devices: 0.01 us -> 0.91 us  [swap_cores(): return lax.ppermute(value, 'row', [(i, i ^ 1) for i in range(N_ROW)])]
    ppermute x7, waiting for transfers between devices: 0.9 us -> 0.02 us  [shards(): before = lax.ppermute(sent, 'row', [(step, step + 1)])]
  transfers between devices with their start and end apart: 23 -> 23, of which waited for: 10 -> 9; matrix products, arithmetic and copies ran while one was open for 0% -> 0% of each run, Pallas kernels for 10% -> 13%
where the time goes in v2:
time: 77.3 us; the launch traced here: 77.1 us
  starting transfers between devices  36.4 us (47%)
  Pallas kernels  19.8 us (26%)
  waiting for transfers between devices  19.5 us (25%)
  between operations  1.22 us (2%)
    ppermute x12, starting transfers between devices, turned_cols(): return lax.ppermute(value, 'col', pairs)  19.1 us
    ppermute x12, waiting for transfers between devices, turned_cols(): return lax.ppermute(value, 'col', pairs)  17.7 us
    ppermute x3, starting transfers between devices, chip_shift(): lax.ppermute(value, 'row', [(2 * a + c, 2 * ((a + k) % SIDE) + c) for a i...  11.6 us
    ppermute x7, starting transfers between devices, shards(): before = lax.ppermute(sent, 'row', [(step, step + 1)])  5.39 us
    pallas_call x1, Pallas kernels, final_second(): pl.pallas_call(body, in_specs=[vmem()] * 4, out_specs=hbm(), scratch_shap...  3.98 us
    pallas_call x1, Pallas kernels, prep_first(): pl.pallas_call(first_body, in_specs=[hbm()] * 3, out_specs=[vmem()] * 5,...  3.58 us
    pallas_call x1, Pallas kernels, build(): pl.pallas_call(build_body, in_specs=[vmem()] * 5, out_specs=vmem(), input...  2.33 us
    pallas_call x4, Pallas kernels, product_own(): pl.pallas_call(body, in_specs=[vmem()] * (2 + len(more)), out_specs=vmem(...  2.25 us
  transfers between devices with their start and end apart: 23, of which 9 were waited for; matrix products, arithmetic and copies ran while one was open for 0% of the time, Pallas kernels for 13%

profile of v2, /device:TPU:0, one launch (start us, length us, event | category | flops | bytes accessed | tf_op | source)
XLA Modules:
  0.0 77.1 jit_solution(16561561189455869805)
XLA Ops:
  0.0 3.6 %prep_first.1 = (bf16[32,1024]{1,0:T(8,128)(2,1)S(1)}, bf16[1024,1024]{1,0:T(8,128)(2,1)S(1)}, bf16[1024,1024]{1,0:T(8,128)(2,1)S(1)}, bf16[512,1024]{1,0:T(8,128)(2,1)S(1)}, bf16[512,1024]{1,0:T(8,128)(2,1)S(1)}) custom-call(f32[32,1024]{1,0:T(8,128)} %rhs_ref.12, f32[1024,1024]{1,0:T(8,128)} %e_hbm.3, f32[1024,1024]{1,0:T(8,128)} %g_hbm.1), custom_call_target="tpu_custom_call" | custom-call | tf_op jit(solution)/shard_map/prep_first/pallas_call | solution.py:101
  3.6 1.4 %collective-permute-start = (bf16[32,1024]{1,0:T(8,128)(2,1)S(1)}, bf16[32,1024]{1,0:T(8,128)(2,1)S(1)}, u32[]{:S(2)}, u32[]{:S(2)}) collective-permute-start(bf16[32,1024]{1,0:T(8,128)(2,1)S(1)} %get-tuple-element.34._.sent_ref), channel_id=1, source_target_pairs={{0,16},{1,17},{2,18},{3,19},{4,20},{5,21},{6,22},{7,23},{8,24},{9,... | collective-permute-start | bytes 196616 | tf_op jit(solution)/shard_map/ppermute | solution.py:414
  5.0 1.7 %prep_second.1 = (bf16[512,1024]{1,0:T(8,128)(2,1)S(1)}, bf16[512,1024]{1,0:T(8,128)(2,1)S(1)}) custom-call(f32[1024,1024]{1,0:T(8,128)} %e_hbm.3, bf16[32,1024]{1,0:T(8,128)(2,1)S(1)} %get-tuple-element.34._.sent_ref), custom_call_target="tpu_custom_call" | custom-call | tf_op jit(solution)/shard_map/prep_second/pallas_call | solution.py:119
  6.9 0.7 collective-permute-start.1
  8.2 1.1 %pack.1 = bf16[13,16,128]{2,1,0:T(8,128)(2,1)S(1)} custom-call(s32[12]{0:T(128)S(1)} %copy-done.3, s32[12]{0:T(128)S(1)} %copy-done.4, s32[1]{0:T(128)S(6)} %copy.27.count, s32[1,48]{1,0:T(1,128)S(1)} %copy-done.5, bf16[12,16,128]{2,1,0:T(8,128)(2,1)S(1)} %copy-done.2), custom_call_target="tpu_custom_call" | custom-call | tf_op jit(solution)/shard_map/pack/pallas_call | solution.py:216
  9.4 0.7 collective-permute-start.2
  10.1 0.7 collective-permute-start.3
  10.8 4.7 %collective-permute-start.6 = (bf16[13,16,128]{2,1,0:T(8,128)(2,1)S(1)}, bf16[13,16,128]{2,1,0:T(8,128)(2,1)S(1)}, u32[]{:S(2)}, u32[]{:S(2)}) collective-permute-start(bf16[13,16,128]{2,1,0:T(8,128)(2,1)S(1)} %pack.1), channel_id=1, source_target_pairs={{0,3},{1,0},{2,1},{3,2},{4,7},{5,4},{6,5},{7,6},{8,11},{9,8},{10,9... | collective-permute-start | bytes 159752 | tf_op jit(solution)/shard_map/ppermute | solution.py:386
  15.5 1.3 %collective-permute-start.4 = (bf16[13,16,128]{2,1,0:T(8,128)(2,1)S(1)}, bf16[13,16,128]{2,1,0:T(8,128)(2,1)S(1)}, u32[]{:S(2)}, u32[]{:S(2)}) collective-permute-start(bf16[13,16,128]{2,1,0:T(8,128)(2,1)S(1)} %pack.1), channel_id=1, source_target_pairs={{0,1},{1,2},{2,3},{3,0},{4,5},{5,6},{6,7},{7,4},{8,9},{9,10},{10,1... | collective-permute-start | bytes 159752 | tf_op jit(solution)/shard_map/ppermute | solution.py:386
  17.2 3.9 %collective-permute-done.5 = bf16[13,16,128]{2,1,0:T(8,128)(2,1)S(1)} collective-permute-done((bf16[13,16,128]{2,1,0:T(8,128)(2,1)S(1)}, bf16[13,16,128]{2,1,0:T(8,128)(2,1)S(1)}, u32[]{:S(2)}, u32[]{:S(2)}) %collective-permute-start.5) | collective-permute-done | bytes 53280 | tf_op jit(solution)/shard_map/ppermute | solution.py:386
  21.2 0.8 %collective-permute-done.4 = bf16[13,16,128]{2,1,0:T(8,128)(2,1)S(1)} collective-permute-done((bf16[13,16,128]{2,1,0:T(8,128)(2,1)S(1)}, bf16[13,16,128]{2,1,0:T(8,128)(2,1)S(1)}, u32[]{:S(2)}, u32[]{:S(2)}) %collective-permute-start.4) | collective-permute-done | bytes 53280 | tf_op jit(solution)/shard_map/ppermute | solution.py:386
  22.0 2.8 %collective-permute-start.12 = (bf16[4,13,16,128]{3,2,1,0:T(8,128)(2,1)S(1)}, bf16[4,13,16,128]{3,2,1,0:T(8,128)(2,1)S(1)}, u32[]{:S(2)}, u32[]{:S(2)}) collective-permute-start(bf16[4,13,16,128]{3,2,1,0:T(8,128)(2,1)S(1)} %pad_maximum_fusion.1.c0), channel_id=1, source_target_pairs={{0,12},{1,13},{2,14},{3,15},{4,0},{5,1},{6,2},{7,3},{8,4},{9,5},{1... | collective-permute-start | bytes 638984 | tf_op jit(solution)/shard_map/ppermute | solution.py:386
  24.8 0.7 collective-permute-start.7
  25.5 0.9 %collective-permute-start.11 = (bf16[4,13,16,128]{3,2,1,0:T(8,128)(2,1)S(1)}, bf16[4,13,16,128]{3,2,1,0:T(8,128)(2,1)S(1)}, u32[]{:S(2)}, u32[]{:S(2)}) collective-permute-start(bf16[4,13,16,128]{3,2,1,0:T(8,128)(2,1)S(1)} %pad_maximum_fusion.1.c0), channel_id=1, source_target_pairs={{0,8},{1,9},{2,10},{3,11},{4,12},{5,13},{6,14},{7,15},{8,0},{9,1},... | collective-permute-start | bytes 638984 | tf_op jit(solution)/shard_map/ppermute | solution.py:386
  26.4 0.9 %collective-permute-start.9 = (bf16[4,13,16,128]{3,2,1,0:T(8,128)(2,1)S(1)}, bf16[4,13,16,128]{3,2,1,0:T(8,128)(2,1)S(1)}, u32[]{:S(2)}, u32[]{:S(2)}) collective-permute-start(bf16[4,13,16,128]{3,2,1,0:T(8,128)(2,1)S(1)} %pad_maximum_fusion.1.c0), channel_id=1, source_target_pairs={{0,4},{1,5},{2,6},{3,7},{4,8},{5,9},{6,10},{7,11},{8,12},{9,13},{1... | collective-permute-start | bytes 638984 | tf_op jit(solution)/shard_map/ppermute | solution.py:386
  27.3 0.7 collective-permute-start.8
  28.2 0.7 collective-permute-start.10
  28.8 0.8 %clear.1.cleared = bf16[8,768,1024]{2,1,0:T(8,128)(2,1)S(1)} custom-call(bf16[32,1024]{1,0:T(8,128)(2,1)S(1)} %shard_map.105._.sent_ref), custom_call_target="tpu_custom_call" | custom-call | tf_op jit(solution)/shard_map/clear/pallas_call | solution.py:231
  29.7 6.0 %collective-permute-start.13 = (bf16[32,1024]{1,0:T(8,128)(2,1)S(1)}, bf16[32,1024]{1,0:T(8,128)(2,1)S(1)}, u32[]{:S(2)}, u32[]{:S(2)}) collective-permute-start(bf16[32,1024]{1,0:T(8,128)(2,1)S(1)} %advance_last.1.x_ref), channel_id=1, source_target_pairs={{0,32},{16,48},{32,64},{48,80},{64,96},{80,112},{96,0},{112,16},{1... | collective-permute-start | bytes 196616 | tf_op jit(solution)/shard_map/ppermute | solution.py:398
  35.7 4.2 %collective-permute-start.15 = (bf16[32,1024]{1,0:T(8,128)(2,1)S(1)}, bf16[32,1024]{1,0:T(8,128)(2,1)S(1)}, u32[]{:S(2)}, u32[]{:S(2)}) collective-permute-start(bf16[32,1024]{1,0:T(8,128)(2,1)S(1)} %advance_last.1.x_ref), channel_id=1, source_target_pairs={{0,96},{16,112},{32,0},{48,16},{64,32},{80,48},{96,64},{112,80},{1... | collective-permute-start | bytes 196616 | tf_op jit(solution)/shard_map/ppermute | solution.py:398
  39.9 1.4 %collective-permute-start.14 = (bf16[32,1024]{1,0:T(8,128)(2,1)S(1)}, bf16[32,1024]{1,0:T(8,128)(2,1)S(1)}, u32[]{:S(2)}, u32[]{:S(2)}) collective-permute-start(bf16[32,1024]{1,0:T(8,128)(2,1)S(1)} %advance_last.1.x_ref), channel_id=1, source_target_pairs={{0,64},{16,80},{32,96},{48,112},{64,0},{80,16},{96,32},{112,48},{1... | collective-permute-start | bytes 196616 | tf_op jit(solution)/shard_map/ppermute | solution.py:398
  41.3 2.3 %build.1.c_ref = bf16[8,768,1024]{2,1,0:T(8,128)(2,1)S(1)} custom-call(bf16[8,768,1024]{2,1,0:T(8,128)(2,1)S(1)} %clear.1.cleared, bf16[4,13,16,128]{3,2,1,0:T(8,128)(2,1)S(1)} %pad_maximum_fusion.1.c0, bf16[4,13,16,128]{3,2,1,0:T(8,128)(2,1)S(1)} %collective-permute-done.9.c1, ...), custom_call_target="tpu_custom_call", output_to_operand_aliasing={{}: (0, {})} | custom-call | tf_op jit(solution)/shard_map/build/pallas_call | solution.py:262
  45.3 0.9 %collective-permute-done.14.x_ref = bf16[32,1024]{1,0:T(8,128)(2,1)S(1)} collective-permute-done((bf16[32,1024]{1,0:T(8,128)(2,1)S(1)}, bf16[32,1024]{1,0:T(8,128)(2,1)S(1)}, u32[]{:S(2)}, u32[]{:S(2)}) %collective-permute-start.14) | collective-permute-done | bytes 65568 | tf_op jit(solution)/shard_map/ppermute | solution.py:398
  47.2 0.9 %collective-permute-done.16.x_ref = bf16[4,32,1024]{2,1,0:T(8,128)(2,1)S(1)} collective-permute-done((bf16[4,32,1024]{2,1,0:T(8,128)(2,1)S(1)}, bf16[4,32,1024]{2,1,0:T(8,128)(2,1)S(1)}, u32[]{:S(2)}, u32[]{:S(2)}) %collective-permute-start.16) | collective-permute-done | bytes 262176 | tf_op jit(solution)/shard_map/ppermute | solution.py:402
  48.1 1.8 %products_other.1 = bf16[32,768]{1,0:T(8,128)(2,1)S(1)} custom-call(bf16[8,768,1024]{2,1,0:T(8,128)(2,1)S(1)} %build.1.c_ref, bf16[4,32,1024]{2,1,0:T(8,128)(2,1)S(1)} %collective-permute-done.16.x_ref, f32[768,32]{1,0:T(8,128)S(1)} %shard_map.109.sum_ref), custom_call_target="tpu_custom_call" | custom-call | tf_op jit(solution)/shard_map/products_other/pallas_call | solution.py:306
  49.9 4.0 %collective-permute-start.19 = (bf16[32,768]{1,0:T(8,128)(2,1)S(1)}, bf16[32,768]{1,0:T(8,128)(2,1)S(1)}, u32[]{:S(2)}, u32[]{:S(2)}) collective-permute-start(bf16[32,768]{1,0:T(8,128)(2,1)S(1)} %products_other.1), channel_id=1, source_target_pairs={{0,3},{1,0},{2,1},{3,2},{4,7},{5,4},{6,5},{7,6},{8,11},{9,8},{10,9... | collective-permute-start | bytes 147464 | tf_op jit(solution)/shard_map/ppermute | solution.py:386
  54.0 1.3 %collective-permute-start.17 = (bf16[32,768]{1,0:T(8,128)(2,1)S(1)}, bf16[32,768]{1,0:T(8,128)(2,1)S(1)}, u32[]{:S(2)}, u32[]{:S(2)}) collective-permute-start(bf16[32,768]{1,0:T(8,128)(2,1)S(1)} %products_other.1), channel_id=1, source_target_pairs={{0,1},{1,2},{2,3},{3,0},{4,5},{5,6},{6,7},{7,4},{8,9},{9,10},{10,1... | collective-permute-start | bytes 147464 | tf_op jit(solution)/shard_map/ppermute | solution.py:386
  55.8 3.7 %collective-permute-done.18 = bf16[32,768]{1,0:T(8,128)(2,1)S(1)} collective-permute-done((bf16[32,768]{1,0:T(8,128)(2,1)S(1)}, bf16[32,768]{1,0:T(8,128)(2,1)S(1)}, u32[]{:S(2)}, u32[]{:S(2)}) %collective-permute-start.18) | collective-permute-done | bytes 49184 | tf_op jit(solution)/shard_map/ppermute | solution.py:386
  59.9 3.2 %collective-permute-start.22 = (bf16[4,32,768]{2,1,0:T(8,128)(2,1)S(1)}, bf16[4,32,768]{2,1,0:T(8,128)(2,1)S(1)}, u32[]{:S(2)}, u32[]{:S(2)}) collective-permute-start(bf16[4,32,768]{2,1,0:T(8,128)(2,1)S(1)} %pad_maximum_fusion.2.w0), channel_id=1, source_target_pairs={{0,12},{1,13},{2,14},{3,15},{4,0},{5,1},{6,2},{7,3},{8,4},{9,5},{1... | collective-permute-start | bytes 589832 | tf_op jit(solution)/shard_map/ppermute | solution.py:386
  63.1 7.9 %collective-permute-done.21.w1 = bf16[4,32,768]{2,1,0:T(8,128)(2,1)S(1)} collective-permute-done((bf16[4,32,768]{2,1,0:T(8,128)(2,1)S(1)}, bf16[4,32,768]{2,1,0:T(8,128)(2,1)S(1)}, u32[]{:S(2)}, u32[]{:S(2)}) %collective-permute-start.21) | collective-permute-done | bytes 196640 | tf_op jit(solution)/shard_map/ppermute | solution.py:386
  71.0 1.9 %final_first.1.part_ref = f32[768,4096]{1,0:T(8,128)S(1)} custom-call(bf16[4,32,768]{2,1,0:T(8,128)(2,1)S(1)} %pad_maximum_fusion.2.w0, bf16[4,32,768]{2,1,0:T(8,128)(2,1)S(1)} %collective-permute-done.21.w1, bf16[512,4096]{1,0:T(8,128)(2,1)S(1)} %copy-done, bf16[768,4096]{1,0:T(8,128)(2,1)S(1)} %bitcast.14), custom_call_target="tpu_custom_call" | custom-call | tf_op jit(solution)/shard_map/final_first/pallas_call | solution.py:347
  72.9 4.0 %final_second.1 = bf16[768,4096]{1,0:T(8,128)(2,1)} custom-call(bf16[4,32,768]{2,1,0:T(8,128)(2,1)S(1)} %collective-permute-done.20.w2, bf16[4,32,768]{2,1,0:T(8,128)(2,1)S(1)} %collective-permute-done.22.w3, bf16[512,4096]{1,0:T(8,128)(2,1)S(1)} %copy-done, f32[768,4096]{1,0:T(8,128)S(1)} %final_first.1.part_ref), custom_call_target="tpu_custom_call" | custom-call | tf_op jit(solution)/shard_map/final_second/pallas_call | solution.py:373
  (54 shorter events, 4.5 us)
Async XLA Ops:
  3.6 3.2 %copy-start.1 = (f32[32,1024]{1,0:T(8,128)S(1)}, f32[32,1024]{1,0:T(8,128)}, u32[]{:S(2)}) copy-start(f32[32,1024]{1,0:T(8,128)} %rhs_ref.12) | copy-start | bytes 393220
  3.6 3.2 %collective-permute-start = (bf16[32,1024]{1,0:T(8,128)(2,1)S(1)}, bf16[32,1024]{1,0:T(8,128)(2,1)S(1)}, u32[]{:S(2)}, u32[]{:S(2)}) collective-permute-start(bf16[32,1024]{1,0:T(8,128)(2,1)S(1)} %get-tuple-element.34._.sent_ref), channel_id=1, source_target_pairs={{0,16},{1,17},{2,18},{3,19},{4,20},{5,21},{6,22},{7,23},{8,24},{9,... | collective-permute-start | bytes 196616 | tf_op jit(solution)/shard_map/ppermute | solution.py:414
  6.8 1.4 %copy-start.2 = (bf16[12,16,128]{2,1,0:T(8,128)(2,1)S(1)}, bf16[12,16,128]{2,1,0:T(8,128)(2,1)}, u32[]{:S(2)}) copy-start(bf16[12,16,128]{2,1,0:T(8,128)(2,1)} %coupling_ref) | copy-start | bytes 147460
  6.8 1.4 %copy-start.3 = (s32[12]{0:T(128)S(1)}, s32[12]{0:T(128)}, u32[]{:S(2)}) copy-start(s32[12]{0:T(128)} %blocks.1) | copy-start | bytes 148
  6.8 1.4 %copy-start.4 = (s32[12]{0:T(128)S(1)}, s32[12]{0:T(128)}, u32[]{:S(2)}) copy-start(s32[12]{0:T(128)} %tiles.1) | copy-start | bytes 148
  6.8 1.4 %copy-start.5 = (s32[1,48]{1,0:T(1,128)S(1)}, s32[1,48]{1,0:T(1,128)}, u32[]{:S(2)}) copy-start(s32[1,48]{1,0:T(1,128)} %slots.1) | copy-start | bytes 580
  6.9 2.5 %collective-permute-start.1 = (bf16[32,1024]{1,0:T(8,128)(2,1)S(1)}, bf16[32,1024]{1,0:T(8,128)(2,1)S(1)}, u32[]{:S(2)}, u32[]{:S(2)}) collective-permute-start(bf16[32,1024]{1,0:T(8,128)(2,1)S(1)} %shard_map.100.sent_ref), channel_id=1, source_target_pairs={{16,32},{17,33},{18,34},{19,35},{20,36},{21,37},{22,38},{23,39},{2... | collective-permute-start | bytes 196616 | tf_op jit(solution)/shard_map/ppermute | solution.py:414
  9.4 0.7 collective-permute-start.2
  10.1 11.9 %collective-permute-start.3 = (bf16[32,1024]{1,0:T(8,128)(2,1)S(1)}, bf16[32,1024]{1,0:T(8,128)(2,1)S(1)}, u32[]{:S(2)}, u32[]{:S(2)}) collective-permute-start(bf16[32,1024]{1,0:T(8,128)(2,1)S(1)} %shard_map.102.sent_ref), channel_id=1, source_target_pairs={{48,64},{49,65},{50,66},{51,67},{52,68},{53,69},{54,70},{55,71},{5... | collective-permute-start | bytes 196616 | tf_op jit(solution)/shard_map/ppermute | solution.py:414
  10.8 6.5 %collective-permute-start.6 = (bf16[13,16,128]{2,1,0:T(8,128)(2,1)S(1)}, bf16[13,16,128]{2,1,0:T(8,128)(2,1)S(1)}, u32[]{:S(2)}, u32[]{:S(2)}) collective-permute-start(bf16[13,16,128]{2,1,0:T(8,128)(2,1)S(1)} %pack.1), channel_id=1, source_target_pairs={{0,3},{1,0},{2,1},{3,2},{4,7},{5,4},{6,5},{7,6},{8,11},{9,8},{10,9... | collective-permute-start | bytes 159752 | tf_op jit(solution)/shard_map/ppermute | solution.py:386
  15.4 5.7 %collective-permute-start.5 = (bf16[13,16,128]{2,1,0:T(8,128)(2,1)S(1)}, bf16[13,16,128]{2,1,0:T(8,128)(2,1)S(1)}, u32[]{:S(2)}, u32[]{:S(2)}) collective-permute-start(bf16[13,16,128]{2,1,0:T(8,128)(2,1)S(1)} %pack.1), channel_id=1, source_target_pairs={{0,2},{1,3},{2,0},{3,1},{4,6},{5,7},{6,4},{7,5},{8,10},{9,11},{10,... | collective-permute-start | bytes 159752 | tf_op jit(solution)/shard_map/ppermute | solution.py:386
  15.5 6.5 %collective-permute-start.4 = (bf16[13,16,128]{2,1,0:T(8,128)(2,1)S(1)}, bf16[13,16,128]{2,1,0:T(8,128)(2,1)S(1)}, u32[]{:S(2)}, u32[]{:S(2)}) collective-permute-start(bf16[13,16,128]{2,1,0:T(8,128)(2,1)S(1)} %pack.1), channel_id=1, source_target_pairs={{0,1},{1,2},{2,3},{3,0},{4,5},{5,6},{6,7},{7,4},{8,9},{9,10},{10,1... | collective-permute-start | bytes 159752 | tf_op jit(solution)/shard_map/ppermute | solution.py:386
  22.0 17.9 %collective-permute-start.12 = (bf16[4,13,16,128]{3,2,1,0:T(8,128)(2,1)S(1)}, bf16[4,13,16,128]{3,2,1,0:T(8,128)(2,1)S(1)}, u32[]{:S(2)}, u32[]{:S(2)}) collective-permute-start(bf16[4,13,16,128]{3,2,1,0:T(8,128)(2,1)S(1)} %pad_maximum_fusion.1.c0), channel_id=1, source_target_pairs={{0,12},{1,13},{2,14},{3,15},{4,0},{5,1},{6,2},{7,3},{8,4},{9,5},{1... | collective-permute-start | bytes 638984 | tf_op jit(solution)/shard_map/ppermute | solution.py:386
  24.8 2.4 %collective-permute-start.7 = (bf16[32,1024]{1,0:T(8,128)(2,1)S(1)}, bf16[32,1024]{1,0:T(8,128)(2,1)S(1)}, u32[]{:S(2)}, u32[]{:S(2)}) collective-permute-start(bf16[32,1024]{1,0:T(8,128)(2,1)S(1)} %shard_map.103.sent_ref), channel_id=1, source_target_pairs={{64,80},{65,81},{66,82},{67,83},{68,84},{69,85},{70,86},{71,87},{7... | collective-permute-start | bytes 196616 | tf_op jit(solution)/shard_map/ppermute | solution.py:414
  25.5 15.8 %collective-permute-start.11 = (bf16[4,13,16,128]{3,2,1,0:T(8,128)(2,1)S(1)}, bf16[4,13,16,128]{3,2,1,0:T(8,128)(2,1)S(1)}, u32[]{:S(2)}, u32[]{:S(2)}) collective-permute-start(bf16[4,13,16,128]{3,2,1,0:T(8,128)(2,1)S(1)} %pad_maximum_fusion.1.c0), channel_id=1, source_target_pairs={{0,8},{1,9},{2,10},{3,11},{4,12},{5,13},{6,14},{7,15},{8,0},{9,1},... | collective-permute-start | bytes 638984 | tf_op jit(solution)/shard_map/ppermute | solution.py:386
  26.4 14.9 %collective-permute-start.9 = (bf16[4,13,16,128]{3,2,1,0:T(8,128)(2,1)S(1)}, bf16[4,13,16,128]{3,2,1,0:T(8,128)(2,1)S(1)}, u32[]{:S(2)}, u32[]{:S(2)}) collective-permute-start(bf16[4,13,16,128]{3,2,1,0:T(8,128)(2,1)S(1)} %pad_maximum_fusion.1.c0), channel_id=1, source_target_pairs={{0,4},{1,5},{2,6},{3,7},{4,8},{5,9},{6,10},{7,11},{8,12},{9,13},{1... | collective-permute-start | bytes 638984 | tf_op jit(solution)/shard_map/ppermute | solution.py:386
  27.3 0.9 %collective-permute-start.8 = (bf16[32,1024]{1,0:T(8,128)(2,1)S(1)}, bf16[32,1024]{1,0:T(8,128)(2,1)S(1)}, u32[]{:S(2)}, u32[]{:S(2)}) collective-permute-start(bf16[32,1024]{1,0:T(8,128)(2,1)S(1)} %shard_map.104.sent_ref), channel_id=1, source_target_pairs={{80,96},{81,97},{82,98},{83,99},{84,100},{85,101},{86,102},{87,103... | collective-permute-start | bytes 196616 | tf_op jit(solution)/shard_map/ppermute | solution.py:414
  28.2 1.5 %collective-permute-start.10 = (bf16[32,1024]{1,0:T(8,128)(2,1)S(1)}, bf16[32,1024]{1,0:T(8,128)(2,1)S(1)}, u32[]{:S(2)}, u32[]{:S(2)}) collective-permute-start(bf16[32,1024]{1,0:T(8,128)(2,1)S(1)} %shard_map.105._.sent_ref), channel_id=1, source_target_pairs={{96,112},{97,113},{98,114},{99,115},{100,116},{101,117},{102,118},... | collective-permute-start | bytes 196616 | tf_op jit(solution)/shard_map/ppermute | solution.py:414
  29.7 14.5 %collective-permute-start.13 = (bf16[32,1024]{1,0:T(8,128)(2,1)S(1)}, bf16[32,1024]{1,0:T(8,128)(2,1)S(1)}, u32[]{:S(2)}, u32[]{:S(2)}) collective-permute-start(bf16[32,1024]{1,0:T(8,128)(2,1)S(1)} %advance_last.1.x_ref), channel_id=1, source_target_pairs={{0,32},{16,48},{32,64},{48,80},{64,96},{80,112},{96,0},{112,16},{1... | collective-permute-start | bytes 196616 | tf_op jit(solution)/shard_map/ppermute | solution.py:398
  35.7 9.0 %collective-permute-start.15 = (bf16[32,1024]{1,0:T(8,128)(2,1)S(1)}, bf16[32,1024]{1,0:T(8,128)(2,1)S(1)}, u32[]{:S(2)}, u32[]{:S(2)}) collective-permute-start(bf16[32,1024]{1,0:T(8,128)(2,1)S(1)} %advance_last.1.x_ref), channel_id=1, source_target_pairs={{0,96},{16,112},{32,0},{48,16},{64,32},{80,48},{96,64},{112,80},{1... | collective-permute-start | bytes 196616 | tf_op jit(solution)/shard_map/ppermute | solution.py:398
  39.9 6.4 %collective-permute-start.14 = (bf16[32,1024]{1,0:T(8,128)(2,1)S(1)}, bf16[32,1024]{1,0:T(8,128)(2,1)S(1)}, u32[]{:S(2)}, u32[]{:S(2)}) collective-permute-start(bf16[32,1024]{1,0:T(8,128)(2,1)S(1)} %advance_last.1.x_ref), channel_id=1, source_target_pairs={{0,64},{16,80},{32,96},{48,112},{64,0},{80,16},{96,32},{112,48},{1... | collective-permute-start | bytes 196616 | tf_op jit(solution)/shard_map/ppermute | solution.py:398
  46.3 1.8 %collective-permute-start.16 = (bf16[4,32,1024]{2,1,0:T(8,128)(2,1)S(1)}, bf16[4,32,1024]{2,1,0:T(8,128)(2,1)S(1)}, u32[]{:S(2)}, u32[]{:S(2)}) collective-permute-start(bf16[4,32,1024]{2,1,0:T(8,128)(2,1)S(1)} %pad_maximum_fusion), channel_id=1, source_target_pairs={{0,16},{16,0},{32,48},{48,32},{64,80},{80,64},{96,112},{112,96},{1... | collective-permute-start | bytes 786440 | tf_op jit(solution)/shard_map/ppermute | solution.py:402
  46.6 24.4 %slice-start = ((s8[6291456]{0:T(1024)(128)(4,1)}), s8[4194304]{0:T(1024)(128)(4,1)S(1)}, s32[]{:S(2)}) async-start(s8[6291456]{0:T(1024)(128)(4,1)} %bitcast.13), calls=%async_computation | async-start | bytes 8388608
  47.2 23.8 %copy-start = (bf16[512,4096]{1,0:T(8,128)(2,1)S(1)}, bf16[512,4096]{1,0:T(8,128)(2,1)}, u32[]{:S(2)}) copy-start(bf16[512,4096]{1,0:T(8,128)(2,1)} %s_ref.3) | copy-start | bytes 12582916
  47.2 23.8 %slice-start.1 = ((s8[6291456]{0:T(1024)(128)(4,1)}), s8[2097152]{0:T(1024)(128)(4,1)S(1)}, s32[]{:S(2)}) async-start(s8[6291456]{0:T(1024)(128)(4,1)} %bitcast.13), calls=%async_computation.1 | async-start | bytes 4194304
  49.9 5.9 %collective-permute-start.19 = (bf16[32,768]{1,0:T(8,128)(2,1)S(1)}, bf16[32,768]{1,0:T(8,128)(2,1)S(1)}, u32[]{:S(2)}, u32[]{:S(2)}) collective-permute-start(bf16[32,768]{1,0:T(8,128)(2,1)S(1)} %products_other.1), channel_id=1, source_target_pairs={{0,3},{1,0},{2,1},{3,2},{4,7},{5,4},{6,5},{7,6},{8,11},{9,8},{10,9... | collective-permute-start | bytes 147464 | tf_op jit(solution)/shard_map/ppermute | solution.py:386
  54.0 5.6 %collective-permute-start.18 = (bf16[32,768]{1,0:T(8,128)(2,1)S(1)}, bf16[32,768]{1,0:T(8,128)(2,1)S(1)}, u32[]{:S(2)}, u32[]{:S(2)}) collective-permute-start(bf16[32,768]{1,0:T(8,128)(2,1)S(1)} %products_other.1), channel_id=1, source_target_pairs={{0,2},{1,3},{2,0},{3,1},{4,6},{5,7},{6,4},{7,5},{8,10},{9,11},{10,... | collective-permute-start | bytes 147464 | tf_op jit(solution)/shard_map/ppermute | solution.py:386
  54.0 5.8 %collective-permute-start.17 = (bf16[32,768]{1,0:T(8,128)(2,1)S(1)}, bf16[32,768]{1,0:T(8,128)(2,1)S(1)}, u32[]{:S(2)}, u32[]{:S(2)}) collective-permute-start(bf16[32,768]{1,0:T(8,128)(2,1)S(1)} %products_other.1), channel_id=1, source_target_pairs={{0,1},{1,2},{2,3},{3,0},{4,5},{5,6},{6,7},{7,4},{8,9},{9,10},{10,1... | collective-permute-start | bytes 147464 | tf_op jit(solution)/shard_map/ppermute | solution.py:386
  59.8 11.2 %collective-permute-start.21 = (bf16[4,32,768]{2,1,0:T(8,128)(2,1)S(1)}, bf16[4,32,768]{2,1,0:T(8,128)(2,1)S(1)}, u32[]{:S(2)}, u32[]{:S(2)}) collective-permute-start(bf16[4,32,768]{2,1,0:T(8,128)(2,1)S(1)} %pad_maximum_fusion.2.w0), channel_id=1, source_target_pairs={{0,4},{1,5},{2,6},{3,7},{4,8},{5,9},{6,10},{7,11},{8,12},{9,13},{1... | collective-permute-start | bytes 589832 | tf_op jit(solution)/shard_map/ppermute | solution.py:386
  59.9 13.0 %collective-permute-start.22 = (bf16[4,32,768]{2,1,0:T(8,128)(2,1)S(1)}, bf16[4,32,768]{2,1,0:T(8,128)(2,1)S(1)}, u32[]{:S(2)}, u32[]{:S(2)}) collective-permute-start(bf16[4,32,768]{2,1,0:T(8,128)(2,1)S(1)} %pad_maximum_fusion.2.w0), channel_id=1, source_target_pairs={{0,12},{1,13},{2,14},{3,15},{4,0},{5,1},{6,2},{7,3},{8,4},{9,5},{1... | collective-permute-start | bytes 589832 | tf_op jit(solution)/shard_map/ppermute | solution.py:386
  63.1 9.8 %collective-permute-start.20 = (bf16[4,32,768]{2,1,0:T(8,128)(2,1)S(1)}, bf16[4,32,768]{2,1,0:T(8,128)(2,1)S(1)}, u32[]{:S(2)}, u32[]{:S(2)}) collective-permute-start(bf16[4,32,768]{2,1,0:T(8,128)(2,1)S(1)} %pad_maximum_fusion.2.w0), channel_id=1, source_target_pairs={{0,8},{1,9},{2,10},{3,11},{4,12},{5,13},{6,14},{7,15},{8,0},{9,1},... | collective-permute-start | bytes 589832 | tf_op jit(solution)/shard_map/ppermute | solution.py:386

commit v3 on v2

--- a/solution.py
+++ b/solution.py
@@ -20,6 +20,7 @@
 SIDE = 4
 CHUNKS = 4
 WIDE = 512
+EDGE = NB // 4
 BF = jnp.bfloat16
 F32 = jnp.float32
 
@@ -86,26 +87,32 @@
     fetch.start()
     g_moves = loads(g_hbm, g_in, sems, 1, 0)
     e_moves = loads(e_hbm, e_in, sems, 1 + CHUNKS, 0)
-    split_arriving(g_moves, g_in, g_high, g_low)
     fetch.wait()
-    sent_ref[...] = with_split(rhs_in[...], g_high[...], g_low[...]).astype(BF)
+    rows = NB // CHUNKS
+    total = None
+    for at, move in enumerate(g_moves):
+        piece = pl.ds(at * rows, rows)
+        move.wait()
+        g_high[piece], g_low[piece] = split(g_in[piece])
+        part = with_split(rhs_in[:, piece], g_high[piece], g_low[piece])
+        total = part if total is None else total + part
+    sent_ref[...] = total.astype(BF)
     split_arriving(e_moves, e_in, e_high, e_low)
 
 
 def second_body(e_hbm, _, e_high, e_low, e_in, sems):
-    split_arriving(loads(e_hbm, e_in, sems, 0, NB // 2), e_in, e_high, e_low)
+    split_arriving(loads(e_hbm, e_in, sems, 0, EDGE), e_in, e_high, e_low)
 
 
 def prep_first(rhs, lower, inverse):
-    half = NB // 2
     return pl.pallas_call(
         first_body,
         in_specs=[hbm()] * 3,
         out_specs=[vmem()] * 5,
-        out_shape=[shape(COLS), shape(NB), shape(NB), shape(half), shape(half)],
+        out_shape=[shape(COLS), shape(NB), shape(NB), shape(EDGE), shape(EDGE)],
         scratch_shapes=[
             pltpu.VMEM((COLS, NB), F32),
-            pltpu.VMEM((half, NB), F32),
+            pltpu.VMEM((EDGE, NB), F32),
             pltpu.VMEM((NB, NB), F32),
             pltpu.SemaphoreType.DMA((1 + 2 * CHUNKS,)),
         ],
@@ -115,27 +122,26 @@
 
 
 def prep_second(lower, earlier):
-    half = NB // 2
     return pl.pallas_call(
         second_body,
         in_specs=[hbm(), pl.BlockSpec(memory_space=pl.ANY)],
         out_specs=[vmem()] * 2,
-        out_shape=[shape(half)] * 2,
-        scratch_shapes=[pltpu.VMEM((half, NB), F32), pltpu.SemaphoreType.DMA((CHUNKS,))],
+        out_shape=[shape(NB - EDGE)] * 2,
+        scratch_shapes=[pltpu.VMEM((NB - EDGE, NB), F32), pltpu.SemaphoreType.DMA((CHUNKS,))],
         compiler_params=small(8),
         name="prep_second",
     )(in_hbm(lower), earlier)
 
 
 def change_body(rhs_ref, g_high, g_low, e0, e1, e2, e3, y_ref, high_ref, low_ref):
-    rows, half = NB // CHUNKS, NB // 2
+    rows = NB // CHUNKS
 
     @pl.when(lax.axis_index("row") == N_ROW - 1)
     def _():
         y_ref[...] = with_split(rhs_ref[...], g_high[...], g_low[...])
         for at in range(CHUNKS):
-            high_e, low_e = (e0, e1) if at * rows < half else (e2, e3)
-            piece = pl.ds(at * rows % half, rows)
+            high_e, low_e = (e0, e1) if at * rows < EDGE else (e2, e3)
+            piece = pl.ds(at * rows - (0 if at * rows < EDGE else EDGE), rows)
             high, low = high_e[piece], low_e[piece]
             change = mm(high, g_high[...]) + mm(high, g_low[...]) + mm(low, g_high[...])
             high_ref[pl.ds(at * rows, rows)], low_ref[pl.ds(at * rows, rows)] = split(-change)
@@ -154,11 +160,9 @@
 
 def advance(step, sent, before, rhs, factors):
     def body(sent_ref, rhs_ref, before_ref, g_high, g_low, e0, e1, e2, e3, out_ref):
-        half = NB // 2
-
         @pl.when(lax.axis_index("row") == step + 1)
         def _():
-            upper, lower = before_ref[:, :half], before_ref[:, half:]
+            upper, lower = before_ref[:, :EDGE], before_ref[:, EDGE:]
             right = rhs_ref[...] - mm(upper, e0[...]) - mm(upper, e1[...]) - mm(lower, e2[...]) - mm(lower, e3[...])
             out_ref[...] = with_split(right, g_high[...], g_low[...]).astype(BF)
 
@@ -436,7 +440,9 @@
         else:
             sent = advance_last(sent, before, *last)
     dense = build([parts[0]] + [after(part, sent) for part in parts[1:]], cleared)
-    line = [sent] + [chip_shift(sent, k) for k in (1, 2, 3)]
+    line = [sent]
+    for k in (1, 2, 3):
+        line.append(chip_shift(sent, k))
     sums = product_own(dense, sent, 0)
     for k in (1, 3, 2):
         line[k] = after(line[k], sums)

time: 77.3 us -> 76.8 us (level)
    pallas_call x1, Pallas kernels: 3.58 us -> 2.79 us  [prep_first(): pl.pallas_call(first_body, in_specs=[hbm()] * 3, out_specs=[vmem()] * 5,...]
  transfers between devices with their start and end apart: 23 -> 23, of which waited for: 9 -> 9; matrix products, arithmetic and copies ran while one was open for 0% -> 0% of each run, Pallas kernels for 13% -> 14%
where the time goes in v3:
time: 76.8 us; the launch traced here: 76.6 us
  starting transfers between devices  36.3 us (47%)
  waiting for transfers between devices  19.5 us (25%)
  Pallas kernels  19.3 us (25%)
  between operations  1.22 us (2%)
    ppermute x12, starting transfers between devices, turned_cols(): return lax.ppermute(value, 'col', pairs)  19.1 us
    ppermute x12, waiting for transfers between devices, turned_cols(): return lax.ppermute(value, 'col', pairs)  17.7 us
    ppermute x3, starting transfers between devices, chip_shift(): lax.ppermute(value, 'row', [(2 * a + c, 2 * ((a + k) % SIDE) + c) for a i...  11.6 us
    ppermute x7, starting transfers between devices, shards(): before = lax.ppermute(sent, 'row', [(step, step + 1)])  5.39 us
    pallas_call x1, Pallas kernels, final_second(): pl.pallas_call(body, in_specs=[vmem()] * 4, out_specs=hbm(), scratch_shap...  3.97 us
    pallas_call x1, Pallas kernels, prep_first(): pl.pallas_call(first_body, in_specs=[hbm()] * 3, out_specs=[vmem()] * 5,...  2.79 us
    pallas_call x1, Pallas kernels, build(): pl.pallas_call(build_body, in_specs=[vmem()] * 5, out_specs=vmem(), input...  2.33 us
    pallas_call x4, Pallas kernels, product_own(): pl.pallas_call(body, in_specs=[vmem()] * (2 + len(more)), out_specs=vmem(...  2.26 us
  transfers between devices with their start and end apart: 23, of which 9 were waited for; matrix products, arithmetic and copies ran while one was open for 0% of the time, Pallas kernels for 14%

profile of v3, /device:TPU:0, one launch (start us, length us, event | category | flops | bytes accessed | tf_op | source)
XLA Modules:
  0.0 76.6 jit_solution(10551413728838713001)
XLA Ops:
  0.0 2.8 %prep_first.1 = (bf16[32,1024]{1,0:T(8,128)(2,1)S(1)}, bf16[1024,1024]{1,0:T(8,128)(2,1)S(1)}, bf16[1024,1024]{1,0:T(8,128)(2,1)S(1)}, bf16[256,1024]{1,0:T(8,128)(2,1)S(1)}, bf16[256,1024]{1,0:T(8,128)(2,1)S(1)}) custom-call(f32[32,1024]{1,0:T(8,128)} %rhs_ref.12, f32[1024,1024]{1,0:T(8,128)} %e_hbm.3, f32[1024,1024]{1,0:T(8,128)} %g_hbm.1), custom_call_target="tpu_custom_call" | custom-call | tf_op jit(solution)/shard_map/prep_first/pallas_call | solution.py:108
  2.8 1.4 %collective-permute-start = (bf16[32,1024]{1,0:T(8,128)(2,1)S(1)}, bf16[32,1024]{1,0:T(8,128)(2,1)S(1)}, u32[]{:S(2)}, u32[]{:S(2)}) collective-permute-start(bf16[32,1024]{1,0:T(8,128)(2,1)S(1)} %get-tuple-element.34._.sent_ref), channel_id=1, source_target_pairs={{0,16},{1,17},{2,18},{3,19},{4,20},{5,21},{6,22},{7,23},{8,24},{9,... | collective-permute-start | bytes 196616 | tf_op jit(solution)/shard_map/ppermute | solution.py:418
  4.2 2.0 %prep_second.1 = (bf16[768,1024]{1,0:T(8,128)(2,1)S(1)}, bf16[768,1024]{1,0:T(8,128)(2,1)S(1)}) custom-call(f32[1024,1024]{1,0:T(8,128)} %e_hbm.3, bf16[32,1024]{1,0:T(8,128)(2,1)S(1)} %get-tuple-element.34._.sent_ref), custom_call_target="tpu_custom_call" | custom-call | tf_op jit(solution)/shard_map/prep_second/pallas_call | solution.py:125
  6.4 0.7 collective-permute-start.1
  7.7 1.1 %pack.1 = bf16[13,16,128]{2,1,0:T(8,128)(2,1)S(1)} custom-call(s32[12]{0:T(128)S(1)} %copy-done.3, s32[12]{0:T(128)S(1)} %copy-done.4, s32[1]{0:T(128)S(6)} %copy.27.count, s32[1,48]{1,0:T(1,128)S(1)} %copy-done.5, bf16[12,16,128]{2,1,0:T(8,128)(2,1)S(1)} %copy-done.2), custom_call_target="tpu_custom_call" | custom-call | tf_op jit(solution)/shard_map/pack/pallas_call | solution.py:220
  8.9 0.7 collective-permute-start.2
  9.6 0.7 collective-permute-start.3
  10.3 4.7 %collective-permute-start.6 = (bf16[13,16,128]{2,1,0:T(8,128)(2,1)S(1)}, bf16[13,16,128]{2,1,0:T(8,128)(2,1)S(1)}, u32[]{:S(2)}, u32[]{:S(2)}) collective-permute-start(bf16[13,16,128]{2,1,0:T(8,128)(2,1)S(1)} %pack.1), channel_id=1, source_target_pairs={{0,3},{1,0},{2,1},{3,2},{4,7},{5,4},{6,5},{7,6},{8,11},{9,8},{10,9... | collective-permute-start | bytes 159752 | tf_op jit(solution)/shard_map/ppermute | solution.py:390
  15.0 1.3 %collective-permute-start.4 = (bf16[13,16,128]{2,1,0:T(8,128)(2,1)S(1)}, bf16[13,16,128]{2,1,0:T(8,128)(2,1)S(1)}, u32[]{:S(2)}, u32[]{:S(2)}) collective-permute-start(bf16[13,16,128]{2,1,0:T(8,128)(2,1)S(1)} %pack.1), channel_id=1, source_target_pairs={{0,1},{1,2},{2,3},{3,0},{4,5},{5,6},{6,7},{7,4},{8,9},{9,10},{10,1... | collective-permute-start | bytes 159752 | tf_op jit(solution)/shard_map/ppermute | solution.py:390
  16.8 3.9 %collective-permute-done.5 = bf16[13,16,128]{2,1,0:T(8,128)(2,1)S(1)} collective-permute-done((bf16[13,16,128]{2,1,0:T(8,128)(2,1)S(1)}, bf16[13,16,128]{2,1,0:T(8,128)(2,1)S(1)}, u32[]{:S(2)}, u32[]{:S(2)}) %collective-permute-start.5) | collective-permute-done | bytes 53280 | tf_op jit(solution)/shard_map/ppermute | solution.py:390
  20.7 0.8 %collective-permute-done.4 = bf16[13,16,128]{2,1,0:T(8,128)(2,1)S(1)} collective-permute-done((bf16[13,16,128]{2,1,0:T(8,128)(2,1)S(1)}, bf16[13,16,128]{2,1,0:T(8,128)(2,1)S(1)}, u32[]{:S(2)}, u32[]{:S(2)}) %collective-permute-start.4) | collective-permute-done | bytes 53280 | tf_op jit(solution)/shard_map/ppermute | solution.py:390
  21.5 2.8 %collective-permute-start.12 = (bf16[4,13,16,128]{3,2,1,0:T(8,128)(2,1)S(1)}, bf16[4,13,16,128]{3,2,1,0:T(8,128)(2,1)S(1)}, u32[]{:S(2)}, u32[]{:S(2)}) collective-permute-start(bf16[4,13,16,128]{3,2,1,0:T(8,128)(2,1)S(1)} %pad_maximum_fusion.1.c0), channel_id=1, source_target_pairs={{0,12},{1,13},{2,14},{3,15},{4,0},{5,1},{6,2},{7,3},{8,4},{9,5},{1... | collective-permute-start | bytes 638984 | tf_op jit(solution)/shard_map/ppermute | solution.py:390
  24.4 0.7 collective-permute-start.7
  25.0 0.9 %collective-permute-start.11 = (bf16[4,13,16,128]{3,2,1,0:T(8,128)(2,1)S(1)}, bf16[4,13,16,128]{3,2,1,0:T(8,128)(2,1)S(1)}, u32[]{:S(2)}, u32[]{:S(2)}) collective-permute-start(bf16[4,13,16,128]{3,2,1,0:T(8,128)(2,1)S(1)} %pad_maximum_fusion.1.c0), channel_id=1, source_target_pairs={{0,8},{1,9},{2,10},{3,11},{4,12},{5,13},{6,14},{7,15},{8,0},{9,1},... | collective-permute-start | bytes 638984 | tf_op jit(solution)/shard_map/ppermute | solution.py:390
  25.9 0.9 %collective-permute-start.9 = (bf16[4,13,16,128]{3,2,1,0:T(8,128)(2,1)S(1)}, bf16[4,13,16,128]{3,2,1,0:T(8,128)(2,1)S(1)}, u32[]{:S(2)}, u32[]{:S(2)}) collective-permute-start(bf16[4,13,16,128]{3,2,1,0:T(8,128)(2,1)S(1)} %pad_maximum_fusion.1.c0), channel_id=1, source_target_pairs={{0,4},{1,5},{2,6},{3,7},{4,8},{5,9},{6,10},{7,11},{8,12},{9,13},{1... | collective-permute-start | bytes 638984 | tf_op jit(solution)/shard_map/ppermute | solution.py:390
  26.8 0.7 collective-permute-start.8
  27.7 0.7 collective-permute-start.10
  28.4 0.8 %clear.1.cleared = bf16[8,768,1024]{2,1,0:T(8,128)(2,1)S(1)} custom-call(bf16[32,1024]{1,0:T(8,128)(2,1)S(1)} %shard_map.105._.sent_ref), custom_call_target="tpu_custom_call" | custom-call | tf_op jit(solution)/shard_map/clear/pallas_call | solution.py:235
  29.2 6.0 %collective-permute-start.13 = (bf16[32,1024]{1,0:T(8,128)(2,1)S(1)}, bf16[32,1024]{1,0:T(8,128)(2,1)S(1)}, u32[]{:S(2)}, u32[]{:S(2)}) collective-permute-start(bf16[32,1024]{1,0:T(8,128)(2,1)S(1)} %advance_last.1.x_ref), channel_id=1, source_target_pairs={{0,32},{16,48},{32,64},{48,80},{64,96},{80,112},{96,0},{112,16},{1... | collective-permute-start | bytes 196616 | tf_op jit(solution)/shard_map/ppermute | solution.py:402
  35.2 4.1 %collective-permute-start.15 = (bf16[32,1024]{1,0:T(8,128)(2,1)S(1)}, bf16[32,1024]{1,0:T(8,128)(2,1)S(1)}, u32[]{:S(2)}, u32[]{:S(2)}) collective-permute-start(bf16[32,1024]{1,0:T(8,128)(2,1)S(1)} %advance_last.1.x_ref), channel_id=1, source_target_pairs={{0,96},{16,112},{32,0},{48,16},{64,32},{80,48},{96,64},{112,80},{1... | collective-permute-start | bytes 196616 | tf_op jit(solution)/shard_map/ppermute | solution.py:402
  39.4 1.4 %collective-permute-start.14 = (bf16[32,1024]{1,0:T(8,128)(2,1)S(1)}, bf16[32,1024]{1,0:T(8,128)(2,1)S(1)}, u32[]{:S(2)}, u32[]{:S(2)}) collective-permute-start(bf16[32,1024]{1,0:T(8,128)(2,1)S(1)} %advance_last.1.x_ref), channel_id=1, source_target_pairs={{0,64},{16,80},{32,96},{48,112},{64,0},{80,16},{96,32},{112,48},{1... | collective-permute-start | bytes 196616 | tf_op jit(solution)/shard_map/ppermute | solution.py:402
  40.8 2.3 %build.1.c_ref = bf16[8,768,1024]{2,1,0:T(8,128)(2,1)S(1)} custom-call(bf16[8,768,1024]{2,1,0:T(8,128)(2,1)S(1)} %clear.1.cleared, bf16[4,13,16,128]{3,2,1,0:T(8,128)(2,1)S(1)} %pad_maximum_fusion.1.c0, bf16[4,13,16,128]{3,2,1,0:T(8,128)(2,1)S(1)} %collective-permute-done.9.c1, ...), custom_call_target="tpu_custom_call", output_to_operand_aliasing={{}: (0, {})} | custom-call | tf_op jit(solution)/shard_map/build/pallas_call | solution.py:266
  44.9 0.9 %collective-permute-done.14.x_ref = bf16[32,1024]{1,0:T(8,128)(2,1)S(1)} collective-permute-done((bf16[32,1024]{1,0:T(8,128)(2,1)S(1)}, bf16[32,1024]{1,0:T(8,128)(2,1)S(1)}, u32[]{:S(2)}, u32[]{:S(2)}) %collective-permute-start.14) | collective-permute-done | bytes 65568 | tf_op jit(solution)/shard_map/ppermute | solution.py:402
  46.7 0.9 %collective-permute-done.16.x_ref = bf16[4,32,1024]{2,1,0:T(8,128)(2,1)S(1)} collective-permute-done((bf16[4,32,1024]{2,1,0:T(8,128)(2,1)S(1)}, bf16[4,32,1024]{2,1,0:T(8,128)(2,1)S(1)}, u32[]{:S(2)}, u32[]{:S(2)}) %collective-permute-start.16) | collective-permute-done | bytes 262176 | tf_op jit(solution)/shard_map/ppermute | solution.py:406
  47.6 1.8 %products_other.1 = bf16[32,768]{1,0:T(8,128)(2,1)S(1)} custom-call(bf16[8,768,1024]{2,1,0:T(8,128)(2,1)S(1)} %build.1.c_ref, bf16[4,32,1024]{2,1,0:T(8,128)(2,1)S(1)} %collective-permute-done.16.x_ref, f32[768,32]{1,0:T(8,128)S(1)} %shard_map.109.sum_ref), custom_call_target="tpu_custom_call" | custom-call | tf_op jit(solution)/shard_map/products_other/pallas_call | solution.py:310
  49.4 4.0 %collective-permute-start.19 = (bf16[32,768]{1,0:T(8,128)(2,1)S(1)}, bf16[32,768]{1,0:T(8,128)(2,1)S(1)}, u32[]{:S(2)}, u32[]{:S(2)}) collective-permute-start(bf16[32,768]{1,0:T(8,128)(2,1)S(1)} %products_other.1), channel_id=1, source_target_pairs={{0,3},{1,0},{2,1},{3,2},{4,7},{5,4},{6,5},{7,6},{8,11},{9,8},{10,9... | collective-permute-start | bytes 147464 | tf_op jit(solution)/shard_map/ppermute | solution.py:390
  53.5 1.3 %collective-permute-start.17 = (bf16[32,768]{1,0:T(8,128)(2,1)S(1)}, bf16[32,768]{1,0:T(8,128)(2,1)S(1)}, u32[]{:S(2)}, u32[]{:S(2)}) collective-permute-start(bf16[32,768]{1,0:T(8,128)(2,1)S(1)} %products_other.1), channel_id=1, source_target_pairs={{0,1},{1,2},{2,3},{3,0},{4,5},{5,6},{6,7},{7,4},{8,9},{9,10},{10,1... | collective-permute-start | bytes 147464 | tf_op jit(solution)/shard_map/ppermute | solution.py:390
  55.3 3.7 %collective-permute-done.18 = bf16[32,768]{1,0:T(8,128)(2,1)S(1)} collective-permute-done((bf16[32,768]{1,0:T(8,128)(2,1)S(1)}, bf16[32,768]{1,0:T(8,128)(2,1)S(1)}, u32[]{:S(2)}, u32[]{:S(2)}) %collective-permute-start.18) | collective-permute-done | bytes 49184 | tf_op jit(solution)/shard_map/ppermute | solution.py:390
  59.4 3.2 %collective-permute-start.22 = (bf16[4,32,768]{2,1,0:T(8,128)(2,1)S(1)}, bf16[4,32,768]{2,1,0:T(8,128)(2,1)S(1)}, u32[]{:S(2)}, u32[]{:S(2)}) collective-permute-start(bf16[4,32,768]{2,1,0:T(8,128)(2,1)S(1)} %pad_maximum_fusion.2.w0), channel_id=1, source_target_pairs={{0,12},{1,13},{2,14},{3,15},{4,0},{5,1},{6,2},{7,3},{8,4},{9,5},{1... | collective-permute-start | bytes 589832 | tf_op jit(solution)/shard_map/ppermute | solution.py:390
  62.6 7.9 %collective-permute-done.21.w1 = bf16[4,32,768]{2,1,0:T(8,128)(2,1)S(1)} collective-permute-done((bf16[4,32,768]{2,1,0:T(8,128)(2,1)S(1)}, bf16[4,32,768]{2,1,0:T(8,128)(2,1)S(1)}, u32[]{:S(2)}, u32[]{:S(2)}) %collective-permute-start.21) | collective-permute-done | bytes 196640 | tf_op jit(solution)/shard_map/ppermute | solution.py:390
  70.5 1.9 %final_first.1.part_ref = f32[768,4096]{1,0:T(8,128)S(1)} custom-call(bf16[4,32,768]{2,1,0:T(8,128)(2,1)S(1)} %pad_maximum_fusion.2.w0, bf16[4,32,768]{2,1,0:T(8,128)(2,1)S(1)} %collective-permute-done.21.w1, bf16[512,4096]{1,0:T(8,128)(2,1)S(1)} %copy-done, bf16[768,4096]{1,0:T(8,128)(2,1)S(1)} %bitcast.14), custom_call_target="tpu_custom_call" | custom-call | tf_op jit(solution)/shard_map/final_first/pallas_call | solution.py:351
  72.4 4.0 %final_second.1 = bf16[768,4096]{1,0:T(8,128)(2,1)} custom-call(bf16[4,32,768]{2,1,0:T(8,128)(2,1)S(1)} %collective-permute-done.20.w2, bf16[4,32,768]{2,1,0:T(8,128)(2,1)S(1)} %collective-permute-done.22.w3, bf16[512,4096]{1,0:T(8,128)(2,1)S(1)} %copy-done, f32[768,4096]{1,0:T(8,128)S(1)} %final_first.1.part_ref), custom_call_target="tpu_custom_call" | custom-call | tf_op jit(solution)/shard_map/final_second/pallas_call | solution.py:377
  (54 shorter events, 4.5 us)
Async XLA Ops:
  2.8 3.5 %copy-start.1 = (f32[32,1024]{1,0:T(8,128)S(1)}, f32[32,1024]{1,0:T(8,128)}, u32[]{:S(2)}) copy-start(f32[32,1024]{1,0:T(8,128)} %rhs_ref.12) | copy-start | bytes 393220
  2.8 3.5 %collective-permute-start = (bf16[32,1024]{1,0:T(8,128)(2,1)S(1)}, bf16[32,1024]{1,0:T(8,128)(2,1)S(1)}, u32[]{:S(2)}, u32[]{:S(2)}) collective-permute-start(bf16[32,1024]{1,0:T(8,128)(2,1)S(1)} %get-tuple-element.34._.sent_ref), channel_id=1, source_target_pairs={{0,16},{1,17},{2,18},{3,19},{4,20},{5,21},{6,22},{7,23},{8,24},{9,... | collective-permute-start | bytes 196616 | tf_op jit(solution)/shard_map/ppermute | solution.py:418
  6.3 1.4 %copy-start.2 = (bf16[12,16,128]{2,1,0:T(8,128)(2,1)S(1)}, bf16[12,16,128]{2,1,0:T(8,128)(2,1)}, u32[]{:S(2)}) copy-start(bf16[12,16,128]{2,1,0:T(8,128)(2,1)} %coupling_ref) | copy-start | bytes 147460
  6.3 1.4 %copy-start.3 = (s32[12]{0:T(128)S(1)}, s32[12]{0:T(128)}, u32[]{:S(2)}) copy-start(s32[12]{0:T(128)} %blocks.1) | copy-start | bytes 148
  6.3 1.4 %copy-start.4 = (s32[12]{0:T(128)S(1)}, s32[12]{0:T(128)}, u32[]{:S(2)}) copy-start(s32[12]{0:T(128)} %tiles.1) | copy-start | bytes 148
  6.3 1.4 %copy-start.5 = (s32[1,48]{1,0:T(1,128)S(1)}, s32[1,48]{1,0:T(1,128)}, u32[]{:S(2)}) copy-start(s32[1,48]{1,0:T(1,128)} %slots.1) | copy-start | bytes 580
  6.4 2.5 %collective-permute-start.1 = (bf16[32,1024]{1,0:T(8,128)(2,1)S(1)}, bf16[32,1024]{1,0:T(8,128)(2,1)S(1)}, u32[]{:S(2)}, u32[]{:S(2)}) collective-permute-start(bf16[32,1024]{1,0:T(8,128)(2,1)S(1)} %shard_map.100.sent_ref), channel_id=1, source_target_pairs={{16,32},{17,33},{18,34},{19,35},{20,36},{21,37},{22,38},{23,39},{2... | collective-permute-start | bytes 196616 | tf_op jit(solution)/shard_map/ppermute | solution.py:418
  8.9 0.7 collective-permute-start.2
  9.6 11.9 %collective-permute-start.3 = (bf16[32,1024]{1,0:T(8,128)(2,1)S(1)}, bf16[32,1024]{1,0:T(8,128)(2,1)S(1)}, u32[]{:S(2)}, u32[]{:S(2)}) collective-permute-start(bf16[32,1024]{1,0:T(8,128)(2,1)S(1)} %shard_map.102.sent_ref), channel_id=1, source_target_pairs={{48,64},{49,65},{50,66},{51,67},{52,68},{53,69},{54,70},{55,71},{5... | collective-permute-start | bytes 196616 | tf_op jit(solution)/shard_map/ppermute | solution.py:418
  10.3 6.5 %collective-permute-start.6 = (bf16[13,16,128]{2,1,0:T(8,128)(2,1)S(1)}, bf16[13,16,128]{2,1,0:T(8,128)(2,1)S(1)}, u32[]{:S(2)}, u32[]{:S(2)}) collective-permute-start(bf16[13,16,128]{2,1,0:T(8,128)(2,1)S(1)} %pack.1), channel_id=1, source_target_pairs={{0,3},{1,0},{2,1},{3,2},{4,7},{5,4},{6,5},{7,6},{8,11},{9,8},{10,9... | collective-permute-start | bytes 159752 | tf_op jit(solution)/shard_map/ppermute | solution.py:390
  15.0 5.7 %collective-permute-start.5 = (bf16[13,16,128]{2,1,0:T(8,128)(2,1)S(1)}, bf16[13,16,128]{2,1,0:T(8,128)(2,1)S(1)}, u32[]{:S(2)}, u32[]{:S(2)}) collective-permute-start(bf16[13,16,128]{2,1,0:T(8,128)(2,1)S(1)} %pack.1), channel_id=1, source_target_pairs={{0,2},{1,3},{2,0},{3,1},{4,6},{5,7},{6,4},{7,5},{8,10},{9,11},{10,... | collective-permute-start | bytes 159752 | tf_op jit(solution)/shard_map/ppermute | solution.py:390
  15.0 6.5 %collective-permute-start.4 = (bf16[13,16,128]{2,1,0:T(8,128)(2,1)S(1)}, bf16[13,16,128]{2,1,0:T(8,128)(2,1)S(1)}, u32[]{:S(2)}, u32[]{:S(2)}) collective-permute-start(bf16[13,16,128]{2,1,0:T(8,128)(2,1)S(1)} %pack.1), channel_id=1, source_target_pairs={{0,1},{1,2},{2,3},{3,0},{4,5},{5,6},{6,7},{7,4},{8,9},{9,10},{10,1... | collective-permute-start | bytes 159752 | tf_op jit(solution)/shard_map/ppermute | solution.py:390
  21.5 17.9 %collective-permute-start.12 = (bf16[4,13,16,128]{3,2,1,0:T(8,128)(2,1)S(1)}, bf16[4,13,16,128]{3,2,1,0:T(8,128)(2,1)S(1)}, u32[]{:S(2)}, u32[]{:S(2)}) collective-permute-start(bf16[4,13,16,128]{3,2,1,0:T(8,128)(2,1)S(1)} %pad_maximum_fusion.1.c0), channel_id=1, source_target_pairs={{0,12},{1,13},{2,14},{3,15},{4,0},{5,1},{6,2},{7,3},{8,4},{9,5},{1... | collective-permute-start | bytes 638984 | tf_op jit(solution)/shard_map/ppermute | solution.py:390
  24.4 2.4 %collective-permute-start.7 = (bf16[32,1024]{1,0:T(8,128)(2,1)S(1)}, bf16[32,1024]{1,0:T(8,128)(2,1)S(1)}, u32[]{:S(2)}, u32[]{:S(2)}) collective-permute-start(bf16[32,1024]{1,0:T(8,128)(2,1)S(1)} %shard_map.103.sent_ref), channel_id=1, source_target_pairs={{64,80},{65,81},{66,82},{67,83},{68,84},{69,85},{70,86},{71,87},{7... | collective-permute-start | bytes 196616 | tf_op jit(solution)/shard_map/ppermute | solution.py:418
  25.0 15.8 %collective-permute-start.11 = (bf16[4,13,16,128]{3,2,1,0:T(8,128)(2,1)S(1)}, bf16[4,13,16,128]{3,2,1,0:T(8,128)(2,1)S(1)}, u32[]{:S(2)}, u32[]{:S(2)}) collective-permute-start(bf16[4,13,16,128]{3,2,1,0:T(8,128)(2,1)S(1)} %pad_maximum_fusion.1.c0), channel_id=1, source_target_pairs={{0,8},{1,9},{2,10},{3,11},{4,12},{5,13},{6,14},{7,15},{8,0},{9,1},... | collective-permute-start | bytes 638984 | tf_op jit(solution)/shard_map/ppermute | solution.py:390
  25.9 14.9 %collective-permute-start.9 = (bf16[4,13,16,128]{3,2,1,0:T(8,128)(2,1)S(1)}, bf16[4,13,16,128]{3,2,1,0:T(8,128)(2,1)S(1)}, u32[]{:S(2)}, u32[]{:S(2)}) collective-permute-start(bf16[4,13,16,128]{3,2,1,0:T(8,128)(2,1)S(1)} %pad_maximum_fusion.1.c0), channel_id=1, source_target_pairs={{0,4},{1,5},{2,6},{3,7},{4,8},{5,9},{6,10},{7,11},{8,12},{9,13},{1... | collective-permute-start | bytes 638984 | tf_op jit(solution)/shard_map/ppermute | solution.py:390
  26.8 0.9 %collective-permute-start.8 = (bf16[32,1024]{1,0:T(8,128)(2,1)S(1)}, bf16[32,1024]{1,0:T(8,128)(2,1)S(1)}, u32[]{:S(2)}, u32[]{:S(2)}) collective-permute-start(bf16[32,1024]{1,0:T(8,128)(2,1)S(1)} %shard_map.104.sent_ref), channel_id=1, source_target_pairs={{80,96},{81,97},{82,98},{83,99},{84,100},{85,101},{86,102},{87,103... | collective-permute-start | bytes 196616 | tf_op jit(solution)/shard_map/ppermute | solution.py:418
  27.7 1.5 %collective-permute-start.10 = (bf16[32,1024]{1,0:T(8,128)(2,1)S(1)}, bf16[32,1024]{1,0:T(8,128)(2,1)S(1)}, u32[]{:S(2)}, u32[]{:S(2)}) collective-permute-start(bf16[32,1024]{1,0:T(8,128)(2,1)S(1)} %shard_map.105._.sent_ref), channel_id=1, source_target_pairs={{96,112},{97,113},{98,114},{99,115},{100,116},{101,117},{102,118},... | collective-permute-start | bytes 196616 | tf_op jit(solution)/shard_map/ppermute | solution.py:418
  29.2 14.5 %collective-permute-start.13 = (bf16[32,1024]{1,0:T(8,128)(2,1)S(1)}, bf16[32,1024]{1,0:T(8,128)(2,1)S(1)}, u32[]{:S(2)}, u32[]{:S(2)}) collective-permute-start(bf16[32,1024]{1,0:T(8,128)(2,1)S(1)} %advance_last.1.x_ref), channel_id=1, source_target_pairs={{0,32},{16,48},{32,64},{48,80},{64,96},{80,112},{96,0},{112,16},{1... | collective-permute-start | bytes 196616 | tf_op jit(solution)/shard_map/ppermute | solution.py:402
  35.2 9.0 %collective-permute-start.15 = (bf16[32,1024]{1,0:T(8,128)(2,1)S(1)}, bf16[32,1024]{1,0:T(8,128)(2,1)S(1)}, u32[]{:S(2)}, u32[]{:S(2)}) collective-permute-start(bf16[32,1024]{1,0:T(8,128)(2,1)S(1)} %advance_last.1.x_ref), channel_id=1, source_target_pairs={{0,96},{16,112},{32,0},{48,16},{64,32},{80,48},{96,64},{112,80},{1... | collective-permute-start | bytes 196616 | tf_op jit(solution)/shard_map/ppermute | solution.py:402
  39.4 6.4 %collective-permute-start.14 = (bf16[32,1024]{1,0:T(8,128)(2,1)S(1)}, bf16[32,1024]{1,0:T(8,128)(2,1)S(1)}, u32[]{:S(2)}, u32[]{:S(2)}) collective-permute-start(bf16[32,1024]{1,0:T(8,128)(2,1)S(1)} %advance_last.1.x_ref), channel_id=1, source_target_pairs={{0,64},{16,80},{32,96},{48,112},{64,0},{80,16},{96,32},{112,48},{1... | collective-permute-start | bytes 196616 | tf_op jit(solution)/shard_map/ppermute | solution.py:402
  45.8 1.8 %collective-permute-start.16 = (bf16[4,32,1024]{2,1,0:T(8,128)(2,1)S(1)}, bf16[4,32,1024]{2,1,0:T(8,128)(2,1)S(1)}, u32[]{:S(2)}, u32[]{:S(2)}) collective-permute-start(bf16[4,32,1024]{2,1,0:T(8,128)(2,1)S(1)} %pad_maximum_fusion), channel_id=1, source_target_pairs={{0,16},{16,0},{32,48},{48,32},{64,80},{80,64},{96,112},{112,96},{1... | collective-permute-start | bytes 786440 | tf_op jit(solution)/shard_map/ppermute | solution.py:406
  46.1 24.4 %slice-start = ((s8[6291456]{0:T(1024)(128)(4,1)}), s8[4194304]{0:T(1024)(128)(4,1)S(1)}, s32[]{:S(2)}) async-start(s8[6291456]{0:T(1024)(128)(4,1)} %bitcast.13), calls=%async_computation | async-start | bytes 8388608
  46.7 23.8 %copy-start = (bf16[512,4096]{1,0:T(8,128)(2,1)S(1)}, bf16[512,4096]{1,0:T(8,128)(2,1)}, u32[]{:S(2)}) copy-start(bf16[512,4096]{1,0:T(8,128)(2,1)} %s_ref.3) | copy-start | bytes 12582916
  46.7 23.8 %slice-start.1 = ((s8[6291456]{0:T(1024)(128)(4,1)}), s8[2097152]{0:T(1024)(128)(4,1)S(1)}, s32[]{:S(2)}) async-start(s8[6291456]{0:T(1024)(128)(4,1)} %bitcast.13), calls=%async_computation.1 | async-start | bytes 4194304
  49.4 5.9 %collective-permute-start.19 = (bf16[32,768]{1,0:T(8,128)(2,1)S(1)}, bf16[32,768]{1,0:T(8,128)(2,1)S(1)}, u32[]{:S(2)}, u32[]{:S(2)}) collective-permute-start(bf16[32,768]{1,0:T(8,128)(2,1)S(1)} %products_other.1), channel_id=1, source_target_pairs={{0,3},{1,0},{2,1},{3,2},{4,7},{5,4},{6,5},{7,6},{8,11},{9,8},{10,9... | collective-permute-start | bytes 147464 | tf_op jit(solution)/shard_map/ppermute | solution.py:390
  53.4 5.6 %collective-permute-start.18 = (bf16[32,768]{1,0:T(8,128)(2,1)S(1)}, bf16[32,768]{1,0:T(8,128)(2,1)S(1)}, u32[]{:S(2)}, u32[]{:S(2)}) collective-permute-start(bf16[32,768]{1,0:T(8,128)(2,1)S(1)} %products_other.1), channel_id=1, source_target_pairs={{0,2},{1,3},{2,0},{3,1},{4,6},{5,7},{6,4},{7,5},{8,10},{9,11},{10,... | collective-permute-start | bytes 147464 | tf_op jit(solution)/shard_map/ppermute | solution.py:390
  53.5 5.8 %collective-permute-start.17 = (bf16[32,768]{1,0:T(8,128)(2,1)S(1)}, bf16[32,768]{1,0:T(8,128)(2,1)S(1)}, u32[]{:S(2)}, u32[]{:S(2)}) collective-permute-start(bf16[32,768]{1,0:T(8,128)(2,1)S(1)} %products_other.1), channel_id=1, source_target_pairs={{0,1},{1,2},{2,3},{3,0},{4,5},{5,6},{6,7},{7,4},{8,9},{9,10},{10,1... | collective-permute-start | bytes 147464 | tf_op jit(solution)/shard_map/ppermute | solution.py:390
  59.3 11.2 %collective-permute-start.21 = (bf16[4,32,768]{2,1,0:T(8,128)(2,1)S(1)}, bf16[4,32,768]{2,1,0:T(8,128)(2,1)S(1)}, u32[]{:S(2)}, u32[]{:S(2)}) collective-permute-start(bf16[4,32,768]{2,1,0:T(8,128)(2,1)S(1)} %pad_maximum_fusion.2.w0), channel_id=1, source_target_pairs={{0,4},{1,5},{2,6},{3,7},{4,8},{5,9},{6,10},{7,11},{8,12},{9,13},{1... | collective-permute-start | bytes 589832 | tf_op jit(solution)/shard_map/ppermute | solution.py:390
  59.4 13.0 %collective-permute-start.22 = (bf16[4,32,768]{2,1,0:T(8,128)(2,1)S(1)}, bf16[4,32,768]{2,1,0:T(8,128)(2,1)S(1)}, u32[]{:S(2)}, u32[]{:S(2)}) collective-permute-start(bf16[4,32,768]{2,1,0:T(8,128)(2,1)S(1)} %pad_maximum_fusion.2.w0), channel_id=1, source_target_pairs={{0,12},{1,13},{2,14},{3,15},{4,0},{5,1},{6,2},{7,3},{8,4},{9,5},{1... | collective-permute-start | bytes 589832 | tf_op jit(solution)/shard_map/ppermute | solution.py:390
  62.6 9.8 %collective-permute-start.20 = (bf16[4,32,768]{2,1,0:T(8,128)(2,1)S(1)}, bf16[4,32,768]{2,1,0:T(8,128)(2,1)S(1)}, u32[]{:S(2)}, u32[]{:S(2)}) collective-permute-start(bf16[4,32,768]{2,1,0:T(8,128)(2,1)S(1)} %pad_maximum_fusion.2.w0), channel_id=1, source_target_pairs={{0,8},{1,9},{2,10},{3,11},{4,12},{5,13},{6,14},{7,15},{8,0},{9,1},... | collective-permute-start | bytes 589832 | tf_op jit(solution)/shard_map/ppermute | solution.py:390
